TPU v7x, 32 devices: a whole 2x2x4 slice. The times are simulated.
32 devices in a mesh: seq: 8 (over y, x, core), dp: 4 (over z).
Axes of the slice: x: 2, y: 2, z: 4, core: 2. Of those that a mesh axis runs over, the one named last changes fastest.
Arguments:
- query: bfloat16 [4, 1536, 1280], P('dp', 'seq'), may hold values from -52 to 52, as said below
- keys: bfloat16 [4, 1536, 1280], P('dp', 'seq'), may hold values from -6 to 6, as said below
- values: bfloat16 [4, 1536, 1280], P('dp', 'seq'), may hold values from -6 to 6
- attn: bfloat16 [4, 1536, 1280], P('dp', 'seq'), may hold values from -6 to 6
- d_block: bfloat16 [4, 1536, 1280], P('dp', 'seq'), may hold values from -6 to 6
- w_out: bfloat16 [1280, 1280], P('dp'), may hold values from -0.15625 to 0.15625
Outputs:
- d_query: bfloat16 [4, 1536, 1280], P('dp', 'seq')
- d_keys: bfloat16 [4, 1536, 1280], P('dp', 'seq')
- d_values: bfloat16 [4, 1536, 1280], P('dp', 'seq')
- d_weight: float32 [1280, 1280], P('dp')
Inputs may be any that keep to these rules, and one draw needn't show every extreme that they name: Some query patches may lie along the sum of two keys of the same video. keys has entries of order one.
All inputs are finite; a program needn't handle non-finite values.
Results may differ from a plain program's by a relative error of at most 0.0058.
Values may be sent and summed in bfloat16 or wider, within the bound.
A program may use at most 64 MiB of HBM per device.

v0:
```python
import jax
import jax.numpy as jnp
from jax import lax
from jax.sharding import PartitionSpec as P

HEAD_DIM = 80


def head_backward(query_h, keys_h, values_h, dout_h, delta_h):
    patch_total = query_h.shape[0]
    block_rows = min(512, patch_total)
    while patch_total % block_rows != 0:
        block_rows = block_rows // 2
    block_total = patch_total // block_rows
    score_scale = HEAD_DIM ** (-0.5)
    contract_last = (((1,), (1,)), ((), ()))
    contract_first = (((0,), (0,)), ((), ()))

    def one_block(carry, inputs):
        keys_grad, values_grad = carry
        query_block, dout_block, delta_block = inputs
        scores = (
            lax.dot_general(query_block, keys_h, contract_last, preferred_element_type=jnp.float32)
            * score_scale
        )
        row_max = jnp.max(scores, axis=1, keepdims=True)
        lse = row_max + jnp.log(jnp.sum(jnp.exp(scores - row_max), axis=1, keepdims=True))
        probs = jnp.exp(scores - lse)
        probs_low = probs.astype(jnp.bfloat16)
        values_grad = values_grad + lax.dot_general(
            probs_low, dout_block, contract_first, preferred_element_type=jnp.float32
        )
        d_probs = lax.dot_general(
            dout_block, values_h, contract_last, preferred_element_type=jnp.float32
        )
        d_scores = (score_scale * probs * (d_probs - delta_block[:, None])).astype(jnp.bfloat16)
        query_grad = jnp.dot(d_scores, keys_h, preferred_element_type=jnp.float32)
        keys_grad = keys_grad + lax.dot_general(
            d_scores, query_block, contract_first, preferred_element_type=jnp.float32
        )
        return ((keys_grad, values_grad), query_grad.astype(jnp.bfloat16))

    empty = jnp.zeros((patch_total, HEAD_DIM), jnp.float32)
    blocked = (
        query_h.reshape(block_total, block_rows, HEAD_DIM),
        dout_h.reshape(block_total, block_rows, HEAD_DIM),
        delta_h.reshape(block_total, block_rows),
    )
    (keys_grad, values_grad), query_blocks = lax.scan(one_block, (empty, empty), blocked)
    return (
        query_blocks.reshape(patch_total, HEAD_DIM),
        keys_grad.astype(jnp.bfloat16),
        values_grad.astype(jnp.bfloat16),
    )


def body(query, keys, values, attn, d_block, w_out):
    seq_count = lax.axis_size("seq")
    dp_count = lax.axis_size("dp")
    tok_rows = query.shape[1]
    features = query.shape[2]
    head_here = features // HEAD_DIM // seq_count
    grad_y = d_block.reshape(tok_rows, features)
    attn_rows = attn.reshape(tok_rows, features)
    d_out = lax.dot_general(
        grad_y,
        lax.all_gather(w_out, "dp", axis=0, tiled=True),
        (((1,), (1,)), ((), ())),
        preferred_element_type=jnp.float32,
    ).astype(jnp.bfloat16)

    def split_heads(array):
        return array.reshape(tok_rows, seq_count, head_here, HEAD_DIM)

    query_all, keys_all, values_all, dout_all, output_all = (
        lax.all_to_all(split_heads(query), "seq", split_axis=1, concat_axis=0, tiled=True),
        lax.all_to_all(split_heads(keys), "seq", split_axis=1, concat_axis=0, tiled=True),
        lax.all_to_all(split_heads(values), "seq", split_axis=1, concat_axis=0, tiled=True),
        lax.all_to_all(split_heads(d_out), "seq", split_axis=1, concat_axis=0, tiled=True),
        lax.all_to_all(split_heads(attn_rows), "seq", split_axis=1, concat_axis=0, tiled=True),
    )
    row_terms = jnp.sum(dout_all.astype(jnp.float32) * output_all.astype(jnp.float32), axis=3)
    query_list = []
    keys_list = []
    values_list = []
    for head in range(head_here):
        gradient = head_backward(
            query_all[:, 0, head],
            keys_all[:, 0, head],
            values_all[:, 0, head],
            dout_all[:, 0, head],
            row_terms[:, 0, head],
        )
        query_list.append(gradient[0])
        keys_list.append(gradient[1])
        values_list.append(gradient[2])
    query_heads = jnp.stack(query_list, axis=1)[:, None]
    keys_heads = jnp.stack(keys_list, axis=1)[:, None]
    values_heads = jnp.stack(values_list, axis=1)[:, None]
    query_back, keys_back, values_back = (
        lax.all_to_all(query_heads, "seq", split_axis=0, concat_axis=1, tiled=True),
        lax.all_to_all(keys_heads, "seq", split_axis=0, concat_axis=1, tiled=True),
        lax.all_to_all(values_heads, "seq", split_axis=0, concat_axis=1, tiled=True),
    )
    factor = 1.0 / float(dp_count * tok_rows * seq_count) ** 0.5
    contract_first = (((0,), (0,)), ((), ()))
    partial_rows = lax.psum_scatter(
        lax.dot_general(attn_rows, grad_y, contract_first, preferred_element_type=jnp.float32)
        * factor,
        "dp",
        scatter_dimension=0,
        tiled=True,
    )
    d_weight = lax.psum(partial_rows, "seq")
    shape_out = (1, tok_rows, features)
    return (
        query_back.reshape(shape_out),
        keys_back.reshape(shape_out),
        values_back.reshape(shape_out),
        d_weight,
    )


def solution(mesh):
    return jax.shard_map(
        body,
        mesh=mesh,
        in_specs=(
            P("dp", "seq", None),
            P("dp", "seq", None),
            P("dp", "seq", None),
            P("dp", "seq", None),
            P("dp", "seq", None),
            P("dp", None),
        ),
        out_specs=(P("dp", "seq", None), P("dp", "seq", None), P("dp", "seq", None), P("dp", None)),
        check_vma=False,
    )
```

profile of v0, /device:TPU:1, one launch (start us, length us, event | category | flops | bytes accessed | tf_op | source)
XLA Modules:
  0.0 277.4 jit_solution(8899856098852248446)
XLA Ops:
  7.9 2.1 copy.112
  10.0 5.2 %all-to-all-start = ((bf16[192,8,2,80]{0,3,2,1:T(8,128)(2,1)}), bf16[192,8,2,80]{0,3,2,1:T(8,128)(2,1)S(1)}, u32[]{:S(2)}, u32[]{:S(2)}) async-start(bf16[192,8,2,80]{0,3,2,1:T(8,128)(2,1)} %bitcast), calls=%async_computation | async-start | bytes 1310720 | tf_op jit(solution)/shard_map/all_to_all | solution.py:76
  15.3 3.8 %convolution_multiply_fusion.2 = f32[1280,1280]{1,0:T(8,128)} fusion(bf16[1,192,1280]{2,1,0:T(8,128)(2,1)S(1)} %copy-done.8, bf16[1,192,1280]{2,1,0:T(8,128)(2,1)S(1)} %copy-done), kind=kOutput, calls=%fused_computation.54 | convolution fusion | flops 630784000 | bytes 7536640 | tf_op jit(solution)/shard_map/dot_general | solution.py:108
  20.1 2.1 copy.114
  22.3 2.1 copy.118
  24.4 6.0 %all-to-all-start.1 = ((bf16[192,8,2,80]{0,3,2,1:T(8,128)(2,1)}), bf16[192,8,2,80]{0,3,2,1:T(8,128)(2,1)}, u32[]{:S(2)}, u32[]{:S(2)}) async-start(bf16[192,8,2,80]{0,3,2,1:T(8,128)(2,1)} %bitcast.192), calls=%async_computation.1 | async-start | bytes 1310720 | tf_op jit(solution)/shard_map/all_to_all | solution.py:77
  31.6 1.7 all_to_all.95
  34.3 4.0 %all-to-all-done.1 = bf16[192,8,2,80]{0,3,2,1:T(8,128)(2,1)} async-done(((bf16[192,8,2,80]{0,3,2,1:T(8,128)(2,1)}), bf16[192,8,2,80]{0,3,2,1:T(8,128)(2,1)}, u32[]{:S(2)}, u32[]{:S(2)}) %all-to-all-start.1) | async-done | bytes 491552 | tf_op jit(solution)/shard_map/all_to_all | solution.py:77
  38.4 7.4 %all-to-all-start.3 = ((bf16[192,8,2,80]{0,3,2,1:T(8,128)(2,1)}), bf16[192,8,2,80]{0,3,2,1:T(8,128)(2,1)}, u32[]{:S(2)}, u32[]{:S(2)}) async-start(bf16[192,8,2,80]{0,3,2,1:T(8,128)(2,1)} %bitcast.13), calls=%async_computation.3 | async-start | bytes 1310720 | tf_op jit(solution)/shard_map/all_to_all | solution.py:78
  45.8 1.5 copy.115
  48.5 1.8 slice_bitcast_fusion.3
  50.6 3.1 %all-to-all-done.3 = bf16[192,8,2,80]{0,3,2,1:T(8,128)(2,1)} async-done(((bf16[192,8,2,80]{0,3,2,1:T(8,128)(2,1)}), bf16[192,8,2,80]{0,3,2,1:T(8,128)(2,1)}, u32[]{:S(2)}, u32[]{:S(2)}) %all-to-all-start.3) | async-done | bytes 491552 | tf_op jit(solution)/shard_map/all_to_all | solution.py:78
  53.7 2.3 copy.119
  56.0 2.4 all_to_all.107
  58.4 18.7 %all-gather.2.cloned.1.call-done = bf16[1280,1280]{1,0:T(8,128)(2,1)} async-done(((bf16[320,1280]{1,0:T(8,128)(2,1)}), bf16[1280,1280]{1,0:T(8,128)(2,1)}) %all-gather.2.cloned.1.call-update) | async-done | bytes 3276816 | tf_op jit(solution)/shard_map/all_gather | solution.py:67
  77.1 3.9 %convolution_convert_fusion.2 = bf16[192,1280]{1,0:T(8,128)(2,1)} fusion(bf16[1280,1280]{1,0:T(8,128)(2,1)} %all-gather.2.cloned.1.call-done, bf16[1,192,1280]{2,1,0:T(8,128)(2,1)S(1)} %copy-done), kind=kOutput, calls=%fused_computation.55 | convolution fusion | flops 629391360 | bytes 4259840 | tf_op jit(solution)/shard_map/dot_general | solution.py:65
  81.0 2.1 copy.116
  83.1 4.9 %all-to-all-start.2 = ((bf16[192,8,2,80]{0,3,2,1:T(8,128)(2,1)}), bf16[192,8,2,80]{0,3,2,1:T(8,128)(2,1)}, u32[]{:S(2)}, u32[]{:S(2)}) async-start(bf16[192,8,2,80]{0,3,2,1:T(8,128)(2,1)} %bitcast.193), calls=%async_computation.2 | async-start | bytes 1310720 | tf_op jit(solution)/shard_map/all_to_all | solution.py:79
  88.1 1.8 slice_bitcast_fusion.2
  92.9 1.9 copy.130
  95.7 7.7 %all-to-all-start.4 = ((bf16[192,8,2,80]{0,3,2,1:T(8,128)(2,1)}), bf16[192,8,2,80]{0,3,2,1:T(8,128)(2,1)}, u32[]{:S(2)}, u32[]{:S(2)}) async-start(bf16[192,8,2,80]{0,3,2,1:T(8,128)(2,1)} %bitcast.190), calls=%async_computation.4 | async-start | bytes 1310720 | tf_op jit(solution)/shard_map/all_to_all | solution.py:80
  103.4 2.3 copy.117
  105.7 2.4 all_to_all.103
  108.1 1.8 fusion.45
  109.9 1.9 copy.143
  111.8 1.5 fusion.39
  114.4 31.9 %while.30 = (s32[]{:T(128)}, f32[1536,80]{0,1:T(8,128)S(1)}, f32[1536,80]{0,1:T(8,128)S(1)}, bf16[3,512,80]{1,2,0:T(8,128)(2,1)S(1)}, bf16[3,512,80]{2,1,0:T(8,1...) while((s32[]{:T(128)}, f32[1536,80]{0,1:T(8,128)S(1)}, ...), condition=%wide.region_4.5_spmd.clone, body=%wide.region_1.4_spmd.clone.sunk | while | flops 638328320 | bytes 46932176 | solution.py:49
  114.4 1.6 fusion.91
  116.0 1.7 copy-done.1
  118.3 2.8 %convolution_add_fusion.9 = f32[1536,80]{0,1:T(8,128)S(1)} fusion(f32[512,1536]{1,0:T(8,128)} %copy-done.1, f32[512]{0:T(512)S(1)} %log_add_fusion.4, f32[1536,80]{0,1:T(8,128)S(1)} %get-tuple-element.496, pred[]{:T(512)S(6)} %compare.6, bf16[3,512,80]{2,1,0:T(8,128)(2,1)} %get-tuple-element.511, s32[]{:T(128)} %get-tuple-element.494), kind=kOutput, calls=%fused_computation.7.clone.1 | convolution fusion | flops 127647744 | bytes 4262401 | tf_op jit(solution)/shard_map/while/body/eval_jaxpr/dot_general | solution.py:30
  121.2 1.8 fusion.92
  125.0 1.6 fusion.91
  126.6 1.7 copy-done.1
  128.9 2.9 %convolution_add_fusion.9 = f32[1536,80]{0,1:T(8,128)S(1)} fusion(f32[512,1536]{1,0:T(8,128)} %copy-done.1, f32[512]{0:T(512)S(1)} %log_add_fusion.4, f32[1536,80]{0,1:T(8,128)S(1)} %get-tuple-element.496, pred[]{:T(512)S(6)} %compare.6, bf16[3,512,80]{2,1,0:T(8,128)(2,1)} %get-tuple-element.511, s32[]{:T(128)} %get-tuple-element.494), kind=kOutput, calls=%fused_computation.7.clone.1 | convolution fusion | flops 127647744 | bytes 4262401 | tf_op jit(solution)/shard_map/while/body/eval_jaxpr/dot_general | solution.py:30
  131.9 1.8 fusion.92
  133.7 1.4 convolution_add_fusion.8
  135.7 1.6 fusion.91
  137.2 1.7 copy-done.1
  139.6 2.8 %convolution_add_fusion.9 = f32[1536,80]{0,1:T(8,128)S(1)} fusion(f32[512,1536]{1,0:T(8,128)} %copy-done.1, f32[512]{0:T(512)S(1)} %log_add_fusion.4, f32[1536,80]{0,1:T(8,128)S(1)} %get-tuple-element.496, pred[]{:T(512)S(6)} %compare.6, bf16[3,512,80]{2,1,0:T(8,128)(2,1)} %get-tuple-element.511, s32[]{:T(128)} %get-tuple-element.494), kind=kOutput, calls=%fused_computation.7.clone.1 | convolution fusion | flops 127647744 | bytes 4262401 | tf_op jit(solution)/shard_map/while/body/eval_jaxpr/dot_general | solution.py:30
  142.5 1.8 fusion.92
  147.1 29.2 %while.31 = (s32[]{:T(128)}, f32[1536,80]{0,1:T(8,128)S(1)}, f32[1536,80]{0,1:T(8,128)S(1)}, bf16[3,512,80]{1,2,0:T(8,128)(2,1)S(1)}, bf16[3,512,80]{2,1,0:T(8,1...) while((s32[]{:T(128)}, f32[1536,80]{0,1:T(8,128)S(1)}, ...), condition=%wide.region_8.9_spmd.clone, body=%wide.region_5.8_spmd.clone.sunk | while | flops 638328320 | bytes 48061684 | solution.py:49
  147.1 1.6 fusion.103
  148.8 1.7 copy-done.3
  151.1 2.8 %convolution_add_fusion.11 = f32[1536,80]{0,1:T(8,128)S(1)} fusion(f32[512,1536]{1,0:T(8,128)} %copy-done.3, f32[512]{0:T(512)S(1)} %log_add_fusion.5, f32[1536,80]{0,1:T(8,128)S(1)} %get-tuple-element.463, pred[]{:T(512)S(6)} %compare.7, bf16[3,512,80]{2,1,0:T(8,128)(2,1)S(1)} %copy-done.7, s32[]{:T(128)} %get-tuple-element.461), kind=kOutput, calls=%fused_computation.34.clone.1 | convolution fusion | flops 127647744 | bytes 4261893 | tf_op jit(solution)/shard_map/while/body/eval_jaxpr/dot_general | solution.py:30
  154.8 1.4 convolution_add_fusion.10
  156.9 1.6 fusion.103
  158.5 1.7 copy-done.3
  160.8 2.8 %convolution_add_fusion.11 = f32[1536,80]{0,1:T(8,128)S(1)} fusion(f32[512,1536]{1,0:T(8,128)} %copy-done.3, f32[512]{0:T(512)S(1)} %log_add_fusion.5, f32[1536,80]{0,1:T(8,128)S(1)} %get-tuple-element.463, pred[]{:T(512)S(6)} %compare.7, bf16[3,512,80]{2,1,0:T(8,128)(2,1)S(1)} %copy-done.7, s32[]{:T(128)} %get-tuple-element.461), kind=kOutput, calls=%fused_computation.34.clone.1 | convolution fusion | flops 127647744 | bytes 4261893 | tf_op jit(solution)/shard_map/while/body/eval_jaxpr/dot_general | solution.py:30
  166.6 1.6 fusion.103
  168.2 1.7 copy-done.3
  170.5 2.8 %convolution_add_fusion.11 = f32[1536,80]{0,1:T(8,128)S(1)} fusion(f32[512,1536]{1,0:T(8,128)} %copy-done.3, f32[512]{0:T(512)S(1)} %log_add_fusion.5, f32[1536,80]{0,1:T(8,128)S(1)} %get-tuple-element.463, pred[]{:T(512)S(6)} %compare.7, bf16[3,512,80]{2,1,0:T(8,128)(2,1)S(1)} %copy-done.7, s32[]{:T(128)} %get-tuple-element.461), kind=kOutput, calls=%fused_computation.34.clone.1 | convolution fusion | flops 127647744 | bytes 4261893 | tf_op jit(solution)/shard_map/while/body/eval_jaxpr/dot_general | solution.py:30
  177.4 1.8 copy.137
  179.2 6.4 %all-to-all-start.7 = ((bf16[1536,1,2,80]{3,2,1,0:T(2,128)(2,1)}), bf16[1536,1,2,80]{3,2,1,0:T(2,128)(2,1)S(1)}, u32[]{:S(2)}, u32[]{:S(2)}) async-start(bf16[1536,1,2,80]{3,2,1,0:T(2,128)(2,1)} %copy.137), calls=%async_computation.7 | async-start | bytes 1572864 | tf_op jit(solution)/shard_map/all_to_all | solution.py:103
  185.7 1.8 copy.135
  187.5 7.2 %all-to-all-done.7 = bf16[1536,1,2,80]{3,2,1,0:T(2,128)(2,1)S(1)} async-done(((bf16[1536,1,2,80]{3,2,1,0:T(2,128)(2,1)}), bf16[1536,1,2,80]{3,2,1,0:T(2,128)(2,1)S(1)}, u32[]{:S(2)}, u32[]{:S(2)}) %all-to-all-start.7) | async-done | bytes 491552 | tf_op jit(solution)/shard_map/all_to_all | solution.py:103
  194.7 7.0 %all-to-all-start.6 = ((bf16[1536,1,2,80]{3,2,1,0:T(2,128)(2,1)}), bf16[1536,1,2,80]{3,2,1,0:T(2,128)(2,1)S(1)}, u32[]{:S(2)}, u32[]{:S(2)}) async-start(bf16[1536,1,2,80]{3,2,1,0:T(2,128)(2,1)} %copy.135), calls=%async_computation.6 | async-start | bytes 1572864 | tf_op jit(solution)/shard_map/all_to_all | solution.py:102
  203.6 1.8 copy.132
  205.4 6.3 %all-to-all-done.6 = bf16[1536,1,2,80]{3,2,1,0:T(2,128)(2,1)S(1)} async-done(((bf16[1536,1,2,80]{3,2,1,0:T(2,128)(2,1)}), bf16[1536,1,2,80]{3,2,1,0:T(2,128)(2,1)S(1)}, u32[]{:S(2)}, u32[]{:S(2)}) %all-to-all-start.6) | async-done | bytes 491552 | tf_op jit(solution)/shard_map/all_to_all | solution.py:102
  211.7 7.7 %all-to-all-start.5 = ((bf16[1536,1,2,80]{3,2,1,0:T(2,128)(2,1)}), bf16[1536,1,2,80]{3,2,1,0:T(2,128)(2,1)S(1)}, u32[]{:S(2)}, u32[]{:S(2)}) async-start(bf16[1536,1,2,80]{3,2,1,0:T(2,128)(2,1)} %copy.132), calls=%async_computation.5 | async-start | bytes 1572864 | tf_op jit(solution)/shard_map/all_to_all | solution.py:101
  219.4 1.9 copy.138
  221.3 2.1 copy.141
  225.6 3.3 %all-to-all-done.5 = bf16[1536,1,2,80]{3,2,1,0:T(2,128)(2,1)S(1)} async-done(((bf16[1536,1,2,80]{3,2,1,0:T(2,128)(2,1)}), bf16[1536,1,2,80]{3,2,1,0:T(2,128)(2,1)S(1)}, u32[]{:S(2)}, u32[]{:S(2)}) %all-to-all-start.5) | async-done | bytes 491552 | tf_op jit(solution)/shard_map/all_to_all | solution.py:101
  230.8 37.4 %all-reduce.2.cloned.1.call-done = f32[320,1280]{1,0:T(8,128)} async-done(((f32[320,1280]{1,0:T(8,128)}), f32[320,1280]{1,0:T(8,128)}) %all-reduce.2.cloned.1.call-update) | async-done | bytes 1638416 | tf_op jit(solution)/shard_map/psum | solution.py:114
  268.2 2.7 copy.174
  (118 shorter events, 34.1 us)
Async XLA Ops:
  7.2 8.1 %copy-start = (bf16[1,192,1280]{2,1,0:T(8,128)(2,1)S(1)}, bf16[1,192,1280]{2,1,0:T(8,128)(2,1)}, u32[]{:S(2)}) copy-start(bf16[1,192,1280]{2,1,0:T(8,128)(2,1)} %param.14) | copy-start | bytes 1474564
  7.2 8.1 %copy-start.8 = (bf16[1,192,1280]{2,1,0:T(8,128)(2,1)S(1)}, bf16[1,192,1280]{2,1,0:T(8,128)(2,1)}, u32[]{:S(2)}) copy-start(bf16[1,192,1280]{2,1,0:T(8,128)(2,1)} %param.13) | copy-start | bytes 1474564
  7.2 69.9 %all-gather.2.cloned.1.call-start = ((), (), s32[]{:S(2)}) async-start(), calls=%async_computation.9 | async-start | bytes 4096000 | tf_op jit(solution)/shard_map/all_gather | solution.py:67
  10.0 14.4 %all-to-all-start = ((bf16[192,8,2,80]{0,3,2,1:T(8,128)(2,1)}), bf16[192,8,2,80]{0,3,2,1:T(8,128)(2,1)S(1)}, u32[]{:S(2)}, u32[]{:S(2)}) async-start(bf16[192,8,2,80]{0,3,2,1:T(8,128)(2,1)} %bitcast), calls=%async_computation | async-start | bytes 1310720 | tf_op jit(solution)/shard_map/all_to_all | solution.py:76
  15.2 186.4 %reduce-scatter.2.cloned.1.call-start = ((), (), s32[]{:S(2)}) async-start(), calls=%async_computation.10 | async-start | bytes 8192000 | tf_op jit(solution)/shard_map/reduce_scatter | solution.py:107
  24.4 14.0 %all-to-all-start.1 = ((bf16[192,8,2,80]{0,3,2,1:T(8,128)(2,1)}), bf16[192,8,2,80]{0,3,2,1:T(8,128)(2,1)}, u32[]{:S(2)}, u32[]{:S(2)}) async-start(bf16[192,8,2,80]{0,3,2,1:T(8,128)(2,1)} %bitcast.192), calls=%async_computation.1 | async-start | bytes 1310720 | tf_op jit(solution)/shard_map/all_to_all | solution.py:77
  38.4 15.3 %all-to-all-start.3 = ((bf16[192,8,2,80]{0,3,2,1:T(8,128)(2,1)}), bf16[192,8,2,80]{0,3,2,1:T(8,128)(2,1)}, u32[]{:S(2)}, u32[]{:S(2)}) async-start(bf16[192,8,2,80]{0,3,2,1:T(8,128)(2,1)} %bitcast.13), calls=%async_computation.3 | async-start | bytes 1310720 | tf_op jit(solution)/shard_map/all_to_all | solution.py:78
  83.1 12.6 %all-to-all-start.2 = ((bf16[192,8,2,80]{0,3,2,1:T(8,128)(2,1)}), bf16[192,8,2,80]{0,3,2,1:T(8,128)(2,1)}, u32[]{:S(2)}, u32[]{:S(2)}) async-start(bf16[192,8,2,80]{0,3,2,1:T(8,128)(2,1)} %bitcast.193), calls=%async_computation.2 | async-start | bytes 1310720 | tf_op jit(solution)/shard_map/all_to_all | solution.py:79
  95.7 16.0 %all-to-all-start.4 = ((bf16[192,8,2,80]{0,3,2,1:T(8,128)(2,1)}), bf16[192,8,2,80]{0,3,2,1:T(8,128)(2,1)}, u32[]{:S(2)}, u32[]{:S(2)}) async-start(bf16[192,8,2,80]{0,3,2,1:T(8,128)(2,1)} %bitcast.190), calls=%async_computation.4 | async-start | bytes 1310720 | tf_op jit(solution)/shard_map/all_to_all | solution.py:80
  116.0 1.7 copy-start.1
  118.3 2.9 %copy-start.2 = (f32[512,1536]{1,0:T(8,128)S(1)}, f32[512,1536]{1,0:T(8,128)}, u32[]{:S(2)}) copy-start(f32[512,1536]{1,0:T(8,128)} %copy-done.1) | copy-start | bytes 9437188 | tf_op jit(solution)/shard_map/while
  118.3 2.9 %copy-start.6 = (bf16[1536,80]{1,0:T(8,128)(2,1)S(1)}, bf16[1536,80]{1,0:T(8,128)(2,1)}, u32[]{:S(2)}) copy-start(bf16[1536,80]{1,0:T(8,128)(2,1)} %get-tuple-element.512) | copy-start | bytes 737284 | tf_op jit(solution)/shard_map/while
  126.6 1.7 copy-start.1
  128.9 2.9 %copy-start.2 = (f32[512,1536]{1,0:T(8,128)S(1)}, f32[512,1536]{1,0:T(8,128)}, u32[]{:S(2)}) copy-start(f32[512,1536]{1,0:T(8,128)} %copy-done.1) | copy-start | bytes 9437188 | tf_op jit(solution)/shard_map/while
  128.9 3.0 %copy-start.6 = (bf16[1536,80]{1,0:T(8,128)(2,1)S(1)}, bf16[1536,80]{1,0:T(8,128)(2,1)}, u32[]{:S(2)}) copy-start(bf16[1536,80]{1,0:T(8,128)(2,1)} %get-tuple-element.512) | copy-start | bytes 737284 | tf_op jit(solution)/shard_map/while
  137.2 1.7 copy-start.1
  139.5 2.9 %copy-start.2 = (f32[512,1536]{1,0:T(8,128)S(1)}, f32[512,1536]{1,0:T(8,128)}, u32[]{:S(2)}) copy-start(f32[512,1536]{1,0:T(8,128)} %copy-done.1) | copy-start | bytes 9437188 | tf_op jit(solution)/shard_map/while
  139.5 2.9 %copy-start.6 = (bf16[1536,80]{1,0:T(8,128)(2,1)S(1)}, bf16[1536,80]{1,0:T(8,128)(2,1)}, u32[]{:S(2)}) copy-start(bf16[1536,80]{1,0:T(8,128)(2,1)} %get-tuple-element.512) | copy-start | bytes 737284 | tf_op jit(solution)/shard_map/while
  147.1 4.0 %copy-start.7 = (bf16[3,512,80]{2,1,0:T(8,128)(2,1)S(1)}, bf16[3,512,80]{2,1,0:T(8,128)(2,1)}, u32[]{:S(2)}) copy-start(bf16[3,512,80]{2,1,0:T(8,128)(2,1)} %get-tuple-element.478) | copy-start | bytes 737284 | tf_op jit(solution)/shard_map/while
  148.7 1.7 copy-start.3
  150.5 3.5 %copy-start.5 = (bf16[1536,80]{1,0:T(8,128)(2,1)S(1)}, bf16[1536,80]{1,0:T(8,128)(2,1)}, u32[]{:S(2)}) copy-start(bf16[1536,80]{1,0:T(8,128)(2,1)} %get-tuple-element.479) | copy-start | bytes 737284 | tf_op jit(solution)/shard_map/while
  151.1 2.9 %copy-start.4 = (f32[512,1536]{1,0:T(8,128)S(1)}, f32[512,1536]{1,0:T(8,128)}, u32[]{:S(2)}) copy-start(f32[512,1536]{1,0:T(8,128)} %copy-done.3) | copy-start | bytes 9437188 | tf_op jit(solution)/shard_map/while
  156.8 3.9 %copy-start.7 = (bf16[3,512,80]{2,1,0:T(8,128)(2,1)S(1)}, bf16[3,512,80]{2,1,0:T(8,128)(2,1)}, u32[]{:S(2)}) copy-start(bf16[3,512,80]{2,1,0:T(8,128)(2,1)} %get-tuple-element.478) | copy-start | bytes 737284 | tf_op jit(solution)/shard_map/while
  158.5 1.7 copy-start.3
  160.2 3.5 %copy-start.5 = (bf16[1536,80]{1,0:T(8,128)(2,1)S(1)}, bf16[1536,80]{1,0:T(8,128)(2,1)}, u32[]{:S(2)}) copy-start(bf16[1536,80]{1,0:T(8,128)(2,1)} %get-tuple-element.479) | copy-start | bytes 737284 | tf_op jit(solution)/shard_map/while
  160.8 2.9 %copy-start.4 = (f32[512,1536]{1,0:T(8,128)S(1)}, f32[512,1536]{1,0:T(8,128)}, u32[]{:S(2)}) copy-start(f32[512,1536]{1,0:T(8,128)} %copy-done.3) | copy-start | bytes 9437188 | tf_op jit(solution)/shard_map/while
  166.6 4.0 %copy-start.7 = (bf16[3,512,80]{2,1,0:T(8,128)(2,1)S(1)}, bf16[3,512,80]{2,1,0:T(8,128)(2,1)}, u32[]{:S(2)}) copy-start(bf16[3,512,80]{2,1,0:T(8,128)(2,1)} %get-tuple-element.478) | copy-start | bytes 737284 | tf_op jit(solution)/shard_map/while
  168.2 1.7 copy-start.3
  169.9 3.5 %copy-start.5 = (bf16[1536,80]{1,0:T(8,128)(2,1)S(1)}, bf16[1536,80]{1,0:T(8,128)(2,1)}, u32[]{:S(2)}) copy-start(bf16[1536,80]{1,0:T(8,128)(2,1)} %get-tuple-element.479) | copy-start | bytes 737284 | tf_op jit(solution)/shard_map/while
  170.5 2.9 %copy-start.4 = (f32[512,1536]{1,0:T(8,128)S(1)}, f32[512,1536]{1,0:T(8,128)}, u32[]{:S(2)}) copy-start(f32[512,1536]{1,0:T(8,128)} %copy-done.3) | copy-start | bytes 9437188 | tf_op jit(solution)/shard_map/while
  176.3 9.4 %copy-start.9 = (bf16[1536,1,80]{0,2,1:T(8,128)(2,1)S(1)}, bf16[1536,1,80]{0,2,1:T(8,128)(2,1)}, u32[]{:S(2)}) copy-start(bf16[1536,1,80]{0,2,1:T(8,128)(2,1)} %get-tuple-element.331) | copy-start | bytes 737284
  179.2 15.5 %all-to-all-start.7 = ((bf16[1536,1,2,80]{3,2,1,0:T(2,128)(2,1)}), bf16[1536,1,2,80]{3,2,1,0:T(2,128)(2,1)S(1)}, u32[]{:S(2)}, u32[]{:S(2)}) async-start(bf16[1536,1,2,80]{3,2,1,0:T(2,128)(2,1)} %copy.137), calls=%async_computation.7 | async-start | bytes 1572864 | tf_op jit(solution)/shard_map/all_to_all | solution.py:103
  194.7 17.0 %all-to-all-start.6 = ((bf16[1536,1,2,80]{3,2,1,0:T(2,128)(2,1)}), bf16[1536,1,2,80]{3,2,1,0:T(2,128)(2,1)S(1)}, u32[]{:S(2)}, u32[]{:S(2)}) async-start(bf16[1536,1,2,80]{3,2,1,0:T(2,128)(2,1)} %copy.135), calls=%async_computation.6 | async-start | bytes 1572864 | tf_op jit(solution)/shard_map/all_to_all | solution.py:102
  201.7 66.5 %all-reduce.2.cloned.1.call-start = ((), (), s32[]{:S(2)}) async-start(), calls=%async_computation.11 | async-start | bytes 3276800 | tf_op jit(solution)/shard_map/psum | solution.py:114
  211.7 17.2 %all-to-all-start.5 = ((bf16[1536,1,2,80]{3,2,1,0:T(2,128)(2,1)}), bf16[1536,1,2,80]{3,2,1,0:T(2,128)(2,1)S(1)}, u32[]{:S(2)}, u32[]{:S(2)}) async-start(bf16[1536,1,2,80]{3,2,1,0:T(2,128)(2,1)} %copy.132), calls=%async_computation.5 | async-start | bytes 1572864 | tf_op jit(solution)/shard_map/all_to_all | solution.py:101
Sparse Core Ops, SparseCore 0:
  9.6 67.4 all-gather.1
  79.4 113.7 reduce-scatter.1
  205.7 62.4 all-reduce.1
where the time goes:
time: 281 us; the launch traced here: 277 us
  waiting for transfers between devices  82.5 us (29%)
  local copies, waits for them, and re-layouts  66.9 us (24%)
  matrix products  54.1 us (19%)
  starting transfers between devices  52.5 us (19%)
  between operations  13.9 us (5%)
  other arithmetic  6.97 us (2%)
    psum x1, waiting for transfers between devices, body(): d_weight = lax.psum(partial_rows, 'seq')  37.4 us
    unnamed x22, local copies, waits for them, and re-layouts  23 us
    all_gather x1, waiting for transfers between devices, body(): lax.all_gather(w_out, 'dp', axis=0, tiled=True)  18.7 us
    dot_general x6, matrix products, one_block(): lax.dot_general(probs_low, dout_block, contract_first, preferred_element_...  17 us
    while x42, local copies, waits for them, and re-layouts  10.6 us
    dot_general x6, matrix products, one_block(): lax.dot_general(query_block, keys_h, contract_last, preferred_element_typ...  9.55 us
    dot_general x6, matrix products, one_block(): lax.dot_general(d_scores, query_block, contract_first, preferred_element_...  8.24 us
    dot_general x6, matrix products, one_block(): lax.dot_general(dout_block, values_h, contract_last, preferred_element_ty...  8 us
  transfers between devices with their start and end apart: 11, of which 8 were waited for; matrix products, arithmetic and copies ran while one was open for 39% of the time, Pallas kernels for 0%

commit v1 on v0

v1 whole, which is shorter than its diff:
```python
import functools
import math

import jax
import jax.numpy as jnp
from jax import lax
from jax.experimental import pallas as pl
from jax.experimental.pallas import tpu as pltpu
from jax.sharding import PartitionSpec as P

HEAD_DIM = 80
MESH = pl.DeviceIdType.MESH
VMEM_LIMIT = 60 * 1024 * 1024
LAST = (((1,), (1,)), ((), ()))
FIRST = (((0,), (0,)), ((), ()))


def gather_kernel(
    seq, dp, q_ref, k_ref, v_ref, a_ref, g_ref, w_ref, pack_out, g_out, w_out,
    packed, g_send, g_recv, f_send, w_send, w_recv, p_send, p_recv, local_sem,
):
    s = lax.axis_index("seq")
    d = lax.axis_index("dp")
    ratio = seq // dp
    home = s // ratio
    partner = s + 1 - 2 * (s % 2)
    width = k_ref.shape[1] // seq

    barrier = pltpu.get_barrier_semaphore()
    for step in range(1, seq):
        pl.semaphore_signal(barrier, inc=1, device_id=(lax.rem(s + step, seq), d), device_id_type=MESH)
    for step in range(1, dp):
        pl.semaphore_signal(barrier, inc=1, device_id=(s, lax.rem(d + step, dp)), device_id_type=MESH)
    pl.semaphore_wait(barrier, seq + dp - 2)

    def w_copy(step):
        return pltpu.make_async_remote_copy(
            src_ref=w_ref.at[s % ratio],
            dst_ref=w_out,
            send_sem=w_send.at[step],
            recv_sem=w_recv,
            device_id=(s, lax.rem(d + step, dp)),
            device_id_type=MESH,
        )

    def direct(step):
        return pltpu.make_async_remote_copy(
            src_ref=g_ref,
            dst_ref=g_out.at[s],
            send_sem=g_send.at[step],
            recv_sem=g_recv.at[s],
            device_id=(lax.rem(s + 2 * step, seq), d),
            device_id_type=MESH,
        )

    def forward(step):
        source = lax.rem(s + seq - 2 * step, seq)
        return pltpu.make_async_remote_copy(
            src_ref=g_ref if step == 0 else g_out.at[source],
            dst_ref=g_out.at[source],
            send_sem=f_send.at[step],
            recv_sem=g_recv.at[source],
            device_id=(partner, d),
            device_id_type=MESH,
        )

    def arrived(source):
        pltpu.make_async_remote_copy(
            src_ref=g_ref,
            dst_ref=g_out.at[source],
            send_sem=f_send.at[0],
            recv_sem=g_recv.at[source],
            device_id=(partner, d),
            device_id_type=MESH,
        ).wait_recv()

    def pack_copy(step):
        peer = lax.rem(s + step, seq)
        return pltpu.make_async_remote_copy(
            src_ref=packed.at[peer],
            dst_ref=pack_out.at[s],
            send_sem=p_send.at[step],
            recv_sem=p_recv.at[s],
            device_id=(peer, d),
            device_id_type=MESH,
        )

    own_g = pltpu.make_async_copy(g_ref, g_out.at[s], local_sem.at[0])
    own_w = pltpu.make_async_copy(w_ref.at[s % ratio], w_out, local_sem.at[1])
    own_pack = pltpu.make_async_copy(packed.at[s], pack_out.at[s], local_sem.at[2])

    for step in range(1, seq // 2):
        direct(step).start()
    forward(0).start()
    own_g.start()

    @pl.when(home == d)
    def _():
        for step in range(1, dp):
            w_copy(step).start()
        own_w.start()

    for peer in range(seq):
        for index, ref in enumerate((q_ref, k_ref, v_ref, a_ref)):
            packed[peer, :, index * width : (index + 1) * width] = ref[
                :, peer * width : (peer + 1) * width
            ]
    for step in range(1, seq):
        pack_copy(step).start()
    own_pack.start()

    for step in range(1, seq // 2):
        arrived(lax.rem(s + seq - 2 * step, seq))
        forward(step).start()
    for step in range(seq // 2):
        arrived(lax.rem(partner + seq - 2 * step, seq))
    for step in range(1, seq):
        source = lax.rem(s + seq - step, seq)
        pltpu.make_async_remote_copy(
            src_ref=packed.at[source],
            dst_ref=pack_out.at[source],
            send_sem=p_send.at[step],
            recv_sem=p_recv.at[source],
            device_id=(source, d),
            device_id_type=MESH,
        ).wait_recv()

    @pl.when(home == d)
    def _():
        for step in range(1, dp):
            w_copy(step).wait_send()
        own_w.wait()

    @pl.when(home != d)
    def _():
        w_copy(1).wait_recv()

    own_g.wait()
    own_pack.wait()
    for step in range(1, seq // 2):
        direct(step).wait_send()
    for step in range(seq // 2):
        forward(step).wait_send()
    for step in range(1, seq):
        pack_copy(step).wait_send()


def gather(seq, dp, query, keys, values, attn, grad_y, w_rows):
    rows, features = query.shape
    width = features // seq
    dma = pltpu.SemaphoreType.DMA
    vmem = pl.BlockSpec(memory_space=pltpu.VMEM)
    hbm = pl.BlockSpec(memory_space=pl.ANY)
    return pl.pallas_call(
        functools.partial(gather_kernel, seq, dp),
        out_shape=(
            jax.ShapeDtypeStruct((seq, rows, 4 * width), jnp.bfloat16),
            jax.ShapeDtypeStruct((seq, rows, features), jnp.bfloat16),
            jax.ShapeDtypeStruct((width, features), jnp.bfloat16),
        ),
        in_specs=[vmem] * 6,
        out_specs=(hbm, hbm, hbm),
        scratch_shapes=[
            pltpu.VMEM((seq, rows, 4 * width), jnp.bfloat16),
            dma((seq,)),
            dma((seq,)),
            dma((seq,)),
            dma((dp,)),
            dma(()),
            dma((seq,)),
            dma((seq,)),
            dma((3,)),
        ],
        compiler_params=pltpu.CompilerParams(
            collective_id=0, has_side_effects=True, vmem_limit_bytes=VMEM_LIMIT
        ),
        name="gather_heads",
    )(query, keys, values, attn, grad_y, w_rows)


def attention_kernel(
    heads, block_rows, factor, pack_ref, g_ref, w_ref, out_ref, dw_ref,
    q_s, k_s, v_s, do_s, delta_s, dk_s, dv_s,
):
    total = pack_ref.shape[0]
    width = heads * HEAD_DIM
    scale = HEAD_DIM ** (-0.5)
    to_log2 = scale * math.log2(math.e)

    @pl.loop(0, total // block_rows)
    def _(block):
        rows = pl.ds(pl.multiple_of(block * block_rows, block_rows), block_rows)
        d_out = lax.dot_general(
            g_ref[rows, :], w_ref[...], LAST, preferred_element_type=jnp.float32
        ).astype(jnp.bfloat16)
        for h in range(heads):
            low = h * HEAD_DIM
            q_s[h, rows, :] = pack_ref[rows, low : low + HEAD_DIM]
            k_s[h, rows, :] = pack_ref[rows, width + low : width + low + HEAD_DIM]
            v_s[h, rows, :] = pack_ref[rows, 2 * width + low : 2 * width + low + HEAD_DIM]
            a_h = pack_ref[rows, 3 * width + low : 3 * width + low + HEAD_DIM]
            do_h = d_out[:, low : low + HEAD_DIM]
            do_s[h, rows, :] = do_h
            product = do_h.astype(jnp.float32) * a_h.astype(jnp.float32)
            delta_s[h, block] = jnp.sum(product.T, axis=0, keepdims=True)

    pieces = dw_ref.shape[0]
    piece = dw_ref.shape[1]
    d_weight = lax.dot_general(
        pack_ref[:, 3 * width : 4 * width], g_ref[...], FIRST, preferred_element_type=jnp.float32
    )
    for index in range(pieces):
        dw_ref[index] = (d_weight[index * piece : (index + 1) * piece, :] * factor).astype(
            jnp.bfloat16
        )

    dk_s[...] = jnp.zeros_like(dk_s)
    dv_s[...] = jnp.zeros_like(dv_s)

    @pl.loop(0, total // block_rows)
    def _(block):
        rows = pl.ds(pl.multiple_of(block * block_rows, block_rows), block_rows)
        for h in range(heads):
            q_b = q_s[h, rows, :]
            do_b = do_s[h, rows, :]
            keys = k_s[h]
            scores = lax.dot_general(keys, q_b, LAST, preferred_element_type=jnp.float32)
            top = jnp.max(scores, axis=0, keepdims=True)
            exps = jnp.exp2((scores - top) * to_log2)
            probs = exps * (1.0 / jnp.sum(exps, axis=0, keepdims=True))
            d_probs = lax.dot_general(v_s[h], do_b, LAST, preferred_element_type=jnp.float32)
            d_scores = (probs * (d_probs - delta_s[h, block]) * scale).astype(jnp.bfloat16)
            dv_s[h] += jnp.dot(probs.astype(jnp.bfloat16), do_b, preferred_element_type=jnp.float32)
            dk_s[h] += jnp.dot(d_scores, q_b, preferred_element_type=jnp.float32)
            dq_t = lax.dot_general(keys, d_scores, FIRST, preferred_element_type=jnp.float32)
            out_ref[rows, h * HEAD_DIM : (h + 1) * HEAD_DIM] = dq_t.T.astype(jnp.bfloat16)

    for h in range(heads):
        low = h * HEAD_DIM
        out_ref[:, width + low : width + low + HEAD_DIM] = dk_s[h].astype(jnp.bfloat16)
        out_ref[:, 2 * width + low : 2 * width + low + HEAD_DIM] = dv_s[h].astype(jnp.bfloat16)


def attention(seq, factor, packed, grad_y, w_rows):
    total = packed.shape[0]
    width, features = w_rows.shape
    heads = width // HEAD_DIM
    block_rows = 512
    while total % block_rows:
        block_rows //= 2
    vmem = pl.BlockSpec(memory_space=pltpu.VMEM)
    low = pltpu.VMEM((heads, total, HEAD_DIM), jnp.bfloat16)
    wide = pltpu.VMEM((heads, total, HEAD_DIM), jnp.float32)
    return pl.pallas_call(
        functools.partial(attention_kernel, heads, block_rows, factor),
        out_shape=(
            jax.ShapeDtypeStruct((total, 3 * width), jnp.bfloat16),
            jax.ShapeDtypeStruct((seq, width // seq, features), jnp.bfloat16),
        ),
        in_specs=[vmem] * 3,
        out_specs=(vmem, vmem),
        scratch_shapes=[
            low, low, low, low,
            pltpu.VMEM((heads, total // block_rows, 1, block_rows), jnp.float32),
            wide, wide,
        ],
        compiler_params=pltpu.CompilerParams(vmem_limit_bytes=VMEM_LIMIT),
        name="attention_backward",
    )(packed, grad_y, w_rows)


def scatter_kernel(
    seq, dp, grad_ref, dw_ref, dq_ref, dk_ref, dv_ref, out_ref,
    landed, parts, total, spread, p_send, p_recv, w_send, w_recv, t_send, t_recv, local_sem,
):
    s = lax.axis_index("seq")
    d = lax.axis_index("dp")
    ratio = seq // dp
    home = s // ratio
    slot = d * ratio + s % ratio
    width = dq_ref.shape[1] // seq
    piece = dw_ref.shape[1]

    barrier = pltpu.get_barrier_semaphore()
    for step in range(1, seq):
        pl.semaphore_signal(barrier, inc=1, device_id=(lax.rem(s + step, seq), d), device_id_type=MESH)
    for row in range(dp):
        for column in range(ratio):
            @pl.when(jnp.logical_or(row != d, d * ratio + column != s))
            def _():
                pl.semaphore_signal(
                    barrier, inc=1, device_id=(d * ratio + column, row), device_id_type=MESH
                )

    @pl.when(home == d)
    def _():
        pl.semaphore_wait(barrier, 2 * seq - 2)

    @pl.when(home != d)
    def _():
        pl.semaphore_wait(barrier, 2 * seq - 1)

    def w_copy(peer):
        return pltpu.make_async_remote_copy(
            src_ref=dw_ref.at[peer],
            dst_ref=parts.at[slot],
            send_sem=w_send.at[peer],
            recv_sem=w_recv.at[slot],
            device_id=(peer, home),
            device_id_type=MESH,
        )

    def grad_copy(step):
        peer = lax.rem(s + step, seq)
        return pltpu.make_async_remote_copy(
            src_ref=grad_ref.at[peer],
            dst_ref=landed.at[s],
            send_sem=p_send.at[step],
            recv_sem=p_recv.at[s],
            device_id=(peer, d),
            device_id_type=MESH,
        )

    def spread_copy(step):
        peer = lax.rem(s + step, seq)
        return pltpu.make_async_remote_copy(
            src_ref=total,
            dst_ref=spread.at[s],
            send_sem=t_send.at[step],
            recv_sem=t_recv.at[s],
            device_id=(peer, d),
            device_id_type=MESH,
        )

    own_part = pltpu.make_async_copy(dw_ref.at[s], parts.at[slot], local_sem.at[0])
    own_grad = pltpu.make_async_copy(grad_ref.at[s], landed.at[s], local_sem.at[1])
    for step in range(seq):
        peer = lax.rem(s + step, seq)

        @pl.when(jnp.logical_or(home != d, peer != s))
        def _():
            w_copy(peer).start()

    @pl.when(home == d)
    def _():
        own_part.start()

    for step in range(1, seq):
        grad_copy(step).start()
    own_grad.start()

    for row in range(dp):
        for column in range(ratio):
            source = row * ratio + column

            @pl.when(jnp.logical_or(row != d, d * ratio + column != s))
            def _():
                pltpu.make_async_remote_copy(
                    src_ref=dw_ref.at[0],
                    dst_ref=parts.at[source],
                    send_sem=w_send.at[0],
                    recv_sem=w_recv.at[source],
                    device_id=(d * ratio + column, row),
                    device_id_type=MESH,
                ).wait_recv()

    @pl.when(home == d)
    def _():
        own_part.wait()

    for column in range(ratio):
        value = parts[column].astype(jnp.float32)
        for row in range(1, dp):
            value = value + parts[row * ratio + column].astype(jnp.float32)
        total[column] = value.astype(jnp.bfloat16)
    for step in range(1, seq):
        spread_copy(step).start()
    own_total = pltpu.make_async_copy(total, spread.at[s], local_sem.at[2])
    own_total.start()

    own_grad.wait()
    for step in range(1, seq):
        source = lax.rem(s + seq - step, seq)
        pltpu.make_async_remote_copy(
            src_ref=grad_ref.at[source],
            dst_ref=landed.at[source],
            send_sem=p_send.at[step],
            recv_sem=p_recv.at[source],
            device_id=(source, d),
            device_id_type=MESH,
        ).wait_recv()
    for source in range(seq):
        for index, ref in enumerate((dq_ref, dk_ref, dv_ref)):
            ref[:, source * width : (source + 1) * width] = landed[
                source, :, index * width : (index + 1) * width
            ]

    own_total.wait()
    for step in range(1, seq):
        source = lax.rem(s + seq - step, seq)
        pltpu.make_async_remote_copy(
            src_ref=total,
            dst_ref=spread.at[source],
            send_sem=t_send.at[step],
            recv_sem=t_recv.at[source],
            device_id=(source, d),
            device_id_type=MESH,
        ).wait_recv()
    for source in range(seq):
        for column in range(ratio):
            start = column * width + source * piece
            out_ref[start : start + piece, :] = spread[source, column].astype(jnp.float32)

    for step in range(seq):
        peer = lax.rem(s + step, seq)

        @pl.when(jnp.logical_or(home != d, peer != s))
        def _():
            w_copy(peer).wait_send()

    for step in range(1, seq):
        grad_copy(step).wait_send()
        spread_copy(step).wait_send()


def scatter(seq, dp, grads, dw_parts):
    rows = grads.shape[1]
    piece, features = dw_parts.shape[1:]
    ratio = seq // dp
    dma = pltpu.SemaphoreType.DMA
    vmem = pl.BlockSpec(memory_space=pltpu.VMEM)
    block = jax.ShapeDtypeStruct((rows, features), jnp.bfloat16)
    return pl.pallas_call(
        functools.partial(scatter_kernel, seq, dp),
        out_shape=(
            block, block, block,
            jax.ShapeDtypeStruct((features // dp, features), jnp.float32),
        ),
        in_specs=[vmem] * 2,
        out_specs=(vmem,) * 4,
        scratch_shapes=[
            pltpu.VMEM(grads.shape, jnp.bfloat16),
            pltpu.VMEM((dp * ratio, piece, features), jnp.bfloat16),
            pltpu.VMEM((ratio, piece, features), jnp.bfloat16),
            pltpu.VMEM((seq, ratio, piece, features), jnp.bfloat16),
            dma((seq,)),
            dma((seq,)),
            dma((seq,)),
            dma((dp * ratio,)),
            dma((seq,)),
            dma((seq,)),
            dma((3,)),
        ],
        compiler_params=pltpu.CompilerParams(
            collective_id=1, has_side_effects=True, vmem_limit_bytes=VMEM_LIMIT
        ),
        name="scatter_gradients",
    )(grads, dw_parts)


def body(query, keys, values, attn, d_block, w_out):
    seq = lax.axis_size("seq")
    dp = lax.axis_size("dp")
    rows, features = query.shape[1:]
    width = features // seq
    flat = lambda array: array.reshape(rows, features)
    packed, grad_y, w_rows = gather(
        seq, dp, flat(query), flat(keys), flat(values), flat(attn), flat(d_block),
        w_out.reshape(seq // dp, width, features),
    )
    factor = 1.0 / float(dp * rows * seq) ** 0.5
    grads, dw_parts = attention(
        seq, factor,
        packed.reshape(seq * rows, 4 * width),
        grad_y.reshape(seq * rows, features),
        w_rows,
    )
    d_query, d_keys, d_values, d_weight = scatter(
        seq, dp, grads.reshape(seq, rows, 3 * width), dw_parts
    )
    whole = lambda array: array.reshape(1, rows, features)
    return whole(d_query), whole(d_keys), whole(d_values), d_weight


def solution(mesh):
    blocks = P("dp", "seq", None)
    return jax.shard_map(
        body,
        mesh=mesh,
        in_specs=(blocks,) * 5 + (P("dp", None),),
        out_specs=(blocks, blocks, blocks, P("dp", None)),
        check_vma=False,
    )
```

time: 281 us -> 139 us (0.49)
  Pallas kernels: 0 us -> 130 us
  waiting for transfers between devices: 82.5 us -> 0 us
  local copies, waits for them, and re-layouts: 66.9 us -> 6.81 us
  matrix products: 54.1 us -> 0 us
  starting transfers between devices: 52.5 us -> 0 us
  between operations: 13.9 us -> 0.66 us
  other arithmetic: 6.97 us -> 0 us
    pallas_call x0 -> x3, Pallas kernels: none -> 130 us  [the longest x1 53.3 us: scatter(): pl.pallas_call(functools.partial(scatter_kernel, seq, dp), out_shape=(blo...]
    dot_general x32 -> x0, matrix products: 54.1 us -> none  [the longest x6 17 us: one_block(): lax.dot_general(probs_low, dout_block, contract_first, preferred_element_...]
    all_to_all x8 -> x0, starting transfers between devices: 52.4 us -> none  [the longest x1 7.71 us: body(): lax.all_to_all(query_heads, 'seq', split_axis=0, concat_axis=1, tiled=True)]
    psum x1 -> x0, waiting for transfers between devices: 37.4 us -> none  [body(): d_weight = lax.psum(partial_rows, 'seq')]
    all_to_all x8 -> x0, waiting for transfers between devices: 25 us -> none  [the longest x1 7.23 us: body(): lax.all_to_all(values_heads, 'seq', split_axis=0, concat_axis=1, tiled=True)]
    all_to_all x12 -> x0, local copies, waits for them, and re-layouts: 19.1 us -> none  [the longest x2 4.68 us: body(): lax.all_to_all(split_heads(values), 'seq', split_axis=1, concat_axis=0, t...]
    all_gather x1 -> x0, waiting for transfers between devices: 18.7 us -> none  [body(): lax.all_gather(w_out, 'dp', axis=0, tiled=True)]
    unnamed x22 -> x6, local copies, waits for them, and re-layouts: 23 us -> 6.81 us
  transfers between devices with their start and end apart: 11 -> 0, of which waited for: 8 -> 0; matrix products, arithmetic and copies ran while one was open for 39% -> 0% of each run, Pallas kernels for 0% -> 0%
where the time goes in v1:
time: 139 us; the launch traced here: 138 us
  Pallas kernels  130 us (94%)
  local copies, waits for them, and re-layouts  6.81 us (5%)
    pallas_call x1, Pallas kernels, scatter(): pl.pallas_call(functools.partial(scatter_kernel, seq, dp), out_shape=(blo...  53.3 us
    pallas_call x1, Pallas kernels, gather(): pl.pallas_call(functools.partial(gather_kernel, seq, dp), out_shape=(jax....  51 us
    pallas_call x1, Pallas kernels, attention(): pl.pallas_call(functools.partial(attention_kernel, heads, block_rows, fac...  25.9 us
    unnamed x6, local copies, waits for them, and re-layouts  6.81 us

profile of v1, /device:TPU:1, one launch (start us, length us, event | category | flops | bytes accessed | tf_op | source)
XLA Modules:
  0.0 137.6 jit_solution(636544527580197)
XLA Ops:
  0.6 51.0 %gather_heads.1 = (bf16[8,192,640]{2,1,0:T(8,128)(2,1)}, bf16[8,192,1280]{2,1,0:T(8,128)(2,1)}, bf16[160,1280]{1,0:T(8,128)(2,1)}) custom-call(bf16[192,1280]{1,0:T(8,128)(2,1)} %bitcast.16, bf16[192,1280]{1,0:T(8,128)(2,1)} %bitcast.17, bf16[192,1280]{1,0:T(8,128)(2,1)} %bitcast.18, bf16[192,1280]{1,0:T(8,128)(2,1)} %bitcast.19, ...), custom_call_target="tpu_custom_call" | custom-call | tf_op jit(solution)/shard_map/gather_heads/pallas_call | solution.py:154
  51.6 25.9 %attention_backward.1 = (bf16[1536,480]{1,0:T(8,128)(2,1)}, bf16[8,20,1280]{2,1,0:T(8,128)(2,1)}) custom-call(bf16[1536,640]{1,0:T(8,128)(2,1)} %bitcast.13, bf16[1536,1280]{1,0:T(8,128)(2,1)} %bitcast.12, bf16[160,1280]{1,0:T(8,128)(2,1)} %get-tuple-element.15.w_ref), custom_call_target="tpu_custom_call" | custom-call | tf_op jit(solution)/shard_map/attention_backward/pallas_call | solution.py:254
  77.5 53.3 %scatter_gradients.1 = (bf16[192,1280]{1,0:T(8,128)(2,1)}, bf16[192,1280]{1,0:T(8,128)(2,1)}, bf16[192,1280]{1,0:T(8,128)(2,1)}, f32[320,1280]{1,0:T(8,128)}) custom-call(bf16[8,192,480]{2,1,0:T(8,128)(2,1)} %bitcast.14, bf16[8,20,1280]{2,1,0:T(8,128)(2,1)} %get-tuple-element.17.dw_ref), custom_call_target="tpu_custom_call" | custom-call | tf_op jit(solution)/shard_map/scatter_gradients/pallas_call | solution.py:433
  130.8 0.0 copy-start
  130.8 2.0 %copy.14 = bf16[1,192,1280]{2,1,0:T(8,128)(2,1)} copy(bf16[1,192,1280]{2,1,0:T(8,128)(2,1)} %bitcast.23) | data formatting | bytes 983040
  132.8 1.8 %copy.15 = bf16[1,192,1280]{2,1,0:T(8,128)(2,1)} copy(bf16[1,192,1280]{2,1,0:T(8,128)(2,1)} %bitcast.22) | data formatting | bytes 983040
  134.6 1.8 %copy.16 = bf16[1,192,1280]{2,1,0:T(8,128)(2,1)} copy(bf16[1,192,1280]{2,1,0:T(8,128)(2,1)} %bitcast.21) | data formatting | bytes 983040
  136.5 0.0 copy-done
  136.5 1.2 copy.17
Async XLA Ops:
  130.8 5.7 %copy-start = (f32[320,1280]{1,0:T(8,128)S(1)}, f32[320,1280]{1,0:T(8,128)}, u32[]{:S(2)}) copy-start(f32[320,1280]{1,0:T(8,128)} %get-tuple-element.29) | copy-start | bytes 4915204

commit v2 on v1

v2 whole, which is shorter than its diff:
```python
import functools
import math

import jax
import jax.numpy as jnp
from jax import lax
from jax.experimental import pallas as pl
from jax.experimental.pallas import tpu as pltpu
from jax.sharding import PartitionSpec as P

HEAD_DIM = 80
MESH = pl.DeviceIdType.MESH
VMEM_LIMIT = 60 * 1024 * 1024
LAST = (((1,), (1,)), ((), ()))
FIRST = (((0,), (0,)), ((), ()))


def gather_kernel(
    seq, dp, q_ref, k_ref, v_ref, a_ref, g_ref, w_ref, pack_out, g_out, w_out,
    packed, g_send, g_recv, f_send, w_send, w_recv, p_send, p_recv, local_sem,
):
    s = lax.axis_index("seq")
    d = lax.axis_index("dp")
    ratio = seq // dp
    home = s // ratio
    partner = s + 1 - 2 * (s % 2)
    width = k_ref.shape[1] // seq

    barrier = pltpu.get_barrier_semaphore()
    for step in range(1, seq):
        pl.semaphore_signal(barrier, inc=1, device_id=(lax.rem(s + step, seq), d), device_id_type=MESH)
    for step in range(1, dp):
        pl.semaphore_signal(barrier, inc=1, device_id=(s, lax.rem(d + step, dp)), device_id_type=MESH)
    pl.semaphore_wait(barrier, seq + dp - 2)

    def w_copy(step):
        return pltpu.make_async_remote_copy(
            src_ref=w_ref.at[s % ratio],
            dst_ref=w_out,
            send_sem=w_send.at[step],
            recv_sem=w_recv,
            device_id=(s, lax.rem(d + step, dp)),
            device_id_type=MESH,
        )

    def direct(step):
        return pltpu.make_async_remote_copy(
            src_ref=g_ref,
            dst_ref=g_out.at[s],
            send_sem=g_send.at[step],
            recv_sem=g_recv.at[s],
            device_id=(lax.rem(s + 2 * step, seq), d),
            device_id_type=MESH,
        )

    def forward(step):
        source = lax.rem(s + seq - 2 * step, seq)
        return pltpu.make_async_remote_copy(
            src_ref=g_ref if step == 0 else g_out.at[source],
            dst_ref=g_out.at[source],
            send_sem=f_send.at[step],
            recv_sem=g_recv.at[source],
            device_id=(partner, d),
            device_id_type=MESH,
        )

    def arrived(source):
        pltpu.make_async_remote_copy(
            src_ref=g_ref,
            dst_ref=g_out.at[source],
            send_sem=f_send.at[0],
            recv_sem=g_recv.at[source],
            device_id=(partner, d),
            device_id_type=MESH,
        ).wait_recv()

    def pack_copy(step):
        peer = lax.rem(s + step, seq)
        return pltpu.make_async_remote_copy(
            src_ref=packed.at[peer],
            dst_ref=pack_out.at[s],
            send_sem=p_send.at[step],
            recv_sem=p_recv.at[s],
            device_id=(peer, d),
            device_id_type=MESH,
        )

    own_g = pltpu.make_async_copy(g_ref, g_out.at[s], local_sem.at[0])
    own_w = pltpu.make_async_copy(w_ref.at[s % ratio], w_out, local_sem.at[1])
    own_pack = pltpu.make_async_copy(packed.at[s], pack_out.at[s], local_sem.at[2])

    for step in range(1, seq // 2):
        direct(step).start()
    forward(0).start()
    own_g.start()

    @pl.when(home == d)
    def _():
        for step in range(1, dp):
            w_copy(step).start()
        own_w.start()

    for peer in range(seq):
        for index, ref in enumerate((q_ref, k_ref, v_ref, a_ref)):
            packed[peer, :, index * width : (index + 1) * width] = ref[
                :, peer * width : (peer + 1) * width
            ]
    for step in range(1, seq):
        pack_copy(step).start()
    own_pack.start()

    for step in range(1, seq // 2):
        arrived(lax.rem(s + seq - 2 * step, seq))
        forward(step).start()
    for step in range(seq // 2):
        arrived(lax.rem(partner + seq - 2 * step, seq))
    for step in range(1, seq):
        source = lax.rem(s + seq - step, seq)
        pltpu.make_async_remote_copy(
            src_ref=packed.at[source],
            dst_ref=pack_out.at[source],
            send_sem=p_send.at[step],
            recv_sem=p_recv.at[source],
            device_id=(source, d),
            device_id_type=MESH,
        ).wait_recv()

    @pl.when(home == d)
    def _():
        for step in range(1, dp):
            w_copy(step).wait_send()
        own_w.wait()

    @pl.when(home != d)
    def _():
        w_copy(1).wait_recv()

    own_g.wait()
    own_pack.wait()
    for step in range(1, seq // 2):
        direct(step).wait_send()
    for step in range(seq // 2):
        forward(step).wait_send()
    for step in range(1, seq):
        pack_copy(step).wait_send()


def gather(seq, dp, query, keys, values, attn, grad_y, w_rows):
    rows, features = query.shape
    width = features // seq
    dma = pltpu.SemaphoreType.DMA
    vmem = pl.BlockSpec(memory_space=pltpu.VMEM)
    hbm = pl.BlockSpec(memory_space=pl.ANY)
    return pl.pallas_call(
        functools.partial(gather_kernel, seq, dp),
        out_shape=(
            jax.ShapeDtypeStruct((seq, rows, 4 * width), jnp.bfloat16),
            jax.ShapeDtypeStruct((seq, rows, features), jnp.bfloat16),
            jax.ShapeDtypeStruct((width, features), jnp.bfloat16),
        ),
        in_specs=[vmem] * 6,
        out_specs=(hbm, hbm, hbm),
        scratch_shapes=[
            pltpu.VMEM((seq, rows, 4 * width), jnp.bfloat16),
            dma((seq,)),
            dma((seq,)),
            dma((seq,)),
            dma((dp,)),
            dma(()),
            dma((seq,)),
            dma((seq,)),
            dma((3,)),
        ],
        compiler_params=pltpu.CompilerParams(
            collective_id=0, has_side_effects=True, vmem_limit_bytes=VMEM_LIMIT
        ),
        name="gather_heads",
    )(query, keys, values, attn, grad_y, w_rows)


def backward_kernel(
    seq, dp, heads, block_rows, factor, pack_ref, g_ref, w_ref, landed, spread,
    q_s, k_s, v_s, do_s, delta_s, dk_s, dv_s, grad_s, dw_s, parts, total_s,
    p_send, p_recv, w_send, w_recv, t_send, f_send, t_recv, local_sem,
):
    s = lax.axis_index("seq")
    d = lax.axis_index("dp")
    ratio = seq // dp
    home = s // ratio
    slot = d * ratio + s % ratio
    partner = s + 1 - 2 * (s % 2)
    patches = pack_ref.shape[0]
    rows_here = patches // seq
    width = heads * HEAD_DIM
    scale = HEAD_DIM ** (-0.5)
    to_log2 = scale * math.log2(math.e)

    def w_copy(peer):
        return pltpu.make_async_remote_copy(
            src_ref=dw_s.at[peer],
            dst_ref=parts.at[slot],
            send_sem=w_send.at[peer],
            recv_sem=w_recv.at[slot],
            device_id=(peer, home),
            device_id_type=MESH,
        )

    def grad_copy(h, peer, source):
        start = pl.multiple_of(peer * rows_here, rows_here)
        return pltpu.make_async_remote_copy(
            src_ref=grad_s.at[h, pl.ds(start, rows_here)],
            dst_ref=landed.at[h, source],
            send_sem=p_send.at[h, peer],
            recv_sem=p_recv.at[h, source],
            device_id=(peer, d),
            device_id_type=MESH,
        )

    def own_grad(h):
        start = pl.multiple_of(s * rows_here, rows_here)
        return pltpu.make_async_copy(
            grad_s.at[h, pl.ds(start, rows_here)], landed.at[h, s], local_sem.at[2 + h]
        )

    def direct(step):
        return pltpu.make_async_remote_copy(
            src_ref=total_s,
            dst_ref=spread.at[s],
            send_sem=t_send.at[step],
            recv_sem=t_recv.at[s],
            device_id=(lax.rem(s + 2 * step, seq), d),
            device_id_type=MESH,
        )

    def forward(step):
        source = lax.rem(s + seq - 2 * step, seq)
        return pltpu.make_async_remote_copy(
            src_ref=total_s if step == 0 else spread.at[source],
            dst_ref=spread.at[source],
            send_sem=f_send.at[step],
            recv_sem=t_recv.at[source],
            device_id=(partner, d),
            device_id_type=MESH,
        )

    def arrived(source):
        pltpu.make_async_remote_copy(
            src_ref=total_s,
            dst_ref=spread.at[source],
            send_sem=f_send.at[0],
            recv_sem=t_recv.at[source],
            device_id=(partner, d),
            device_id_type=MESH,
        ).wait_recv()

    own_part = pltpu.make_async_copy(dw_s.at[s], parts.at[slot], local_sem.at[0])
    own_total = pltpu.make_async_copy(total_s, spread.at[s], local_sem.at[1])

    barrier = pltpu.get_barrier_semaphore()
    for step in range(1, seq):
        pl.semaphore_signal(barrier, inc=1, device_id=(lax.rem(s + step, seq), d), device_id_type=MESH)
    for row in range(dp):
        for column in range(ratio):
            @pl.when(jnp.logical_or(row != d, d * ratio + column != s))
            def _():
                pl.semaphore_signal(
                    barrier, inc=1, device_id=(d * ratio + column, row), device_id_type=MESH
                )

    pieces = dw_s.shape[0]
    piece = dw_s.shape[1]
    d_weight = lax.dot_general(
        pack_ref[:, 3 * width : 4 * width], g_ref[...], FIRST, preferred_element_type=jnp.float32
    )
    for index in range(pieces):
        dw_s[index] = (d_weight[index * piece : (index + 1) * piece, :] * factor).astype(
            jnp.bfloat16
        )

    @pl.when(home == d)
    def _():
        pl.semaphore_wait(barrier, 2 * seq - 2)

    @pl.when(home != d)
    def _():
        pl.semaphore_wait(barrier, 2 * seq - 1)

    for step in range(seq):
        peer = lax.rem(s + step, seq)

        @pl.when(jnp.logical_or(home != d, peer != s))
        def _():
            w_copy(peer).start()

    @pl.when(home == d)
    def _():
        own_part.start()

    @pl.loop(0, patches // block_rows)
    def _(block):
        rows = pl.ds(pl.multiple_of(block * block_rows, block_rows), block_rows)
        d_out = lax.dot_general(
            g_ref[rows, :], w_ref[...], LAST, preferred_element_type=jnp.float32
        ).astype(jnp.bfloat16)
        for h in range(heads):
            low = h * HEAD_DIM
            q_s[h, rows, :] = pack_ref[rows, low : low + HEAD_DIM]
            k_s[h, rows, :] = pack_ref[rows, width + low : width + low + HEAD_DIM]
            v_s[h, rows, :] = pack_ref[rows, 2 * width + low : 2 * width + low + HEAD_DIM]
            a_h = pack_ref[rows, 3 * width + low : 3 * width + low + HEAD_DIM]
            do_h = d_out[:, low : low + HEAD_DIM]
            do_s[h, rows, :] = do_h
            product = do_h.astype(jnp.float32) * a_h.astype(jnp.float32)
            delta_s[h, block] = jnp.sum(product.T, axis=0, keepdims=True)

    for h in range(heads):
        dk_s[...] = jnp.zeros_like(dk_s)
        dv_s[...] = jnp.zeros_like(dv_s)

        @pl.loop(0, patches // block_rows)
        def _(block):
            rows = pl.ds(pl.multiple_of(block * block_rows, block_rows), block_rows)
            q_b = q_s[h, rows, :]
            do_b = do_s[h, rows, :]
            keys = k_s[h]
            scores = lax.dot_general(keys, q_b, LAST, preferred_element_type=jnp.float32)
            top = jnp.max(scores, axis=0, keepdims=True)
            exps = jnp.exp2((scores - top) * to_log2)
            probs = exps * (1.0 / jnp.sum(exps, axis=0, keepdims=True))
            d_probs = lax.dot_general(v_s[h], do_b, LAST, preferred_element_type=jnp.float32)
            d_scores = (probs * (d_probs - delta_s[h, block]) * scale).astype(jnp.bfloat16)
            dv_s[...] += jnp.dot(probs.astype(jnp.bfloat16), do_b, preferred_element_type=jnp.float32)
            dk_s[...] += jnp.dot(d_scores, q_b, preferred_element_type=jnp.float32)
            dq_t = lax.dot_general(keys, d_scores, FIRST, preferred_element_type=jnp.float32)
            grad_s[h, rows, 0:HEAD_DIM] = dq_t.T.astype(jnp.bfloat16)

        grad_s[h, :, HEAD_DIM : 2 * HEAD_DIM] = dk_s[...].astype(jnp.bfloat16)
        grad_s[h, :, 2 * HEAD_DIM : 3 * HEAD_DIM] = dv_s[...].astype(jnp.bfloat16)

        if h == 0:
            for row in range(dp):
                for column in range(ratio):
                    source = row * ratio + column

                    @pl.when(jnp.logical_or(row != d, d * ratio + column != s))
                    def _():
                        pltpu.make_async_remote_copy(
                            src_ref=dw_s.at[0],
                            dst_ref=parts.at[source],
                            send_sem=w_send.at[0],
                            recv_sem=w_recv.at[source],
                            device_id=(d * ratio + column, row),
                            device_id_type=MESH,
                        ).wait_recv()

            @pl.when(home == d)
            def _():
                own_part.wait()

            for column in range(ratio):
                value = parts[column].astype(jnp.float32)
                for row in range(1, dp):
                    value = value + parts[row * ratio + column].astype(jnp.float32)
                total_s[column] = value.astype(jnp.bfloat16)

        for step in range(1, seq):
            grad_copy(h, lax.rem(s + step, seq), s).start()
        own_grad(h).start()
        if h == 0:
            for step in range(1, seq // 2):
                direct(step).start()
            forward(0).start()
            own_total.start()

    for step in range(1, seq // 2):
        arrived(lax.rem(s + seq - 2 * step, seq))
        forward(step).start()
    for h in range(heads):
        own_grad(h).wait()
        for step in range(1, seq):
            source = lax.rem(s + seq - step, seq)
            grad_copy(h, source, source).wait_recv()
    for step in range(seq // 2):
        arrived(lax.rem(partner + seq - 2 * step, seq))

    own_total.wait()
    for step in range(seq):
        peer = lax.rem(s + step, seq)

        @pl.when(jnp.logical_or(home != d, peer != s))
        def _():
            w_copy(peer).wait_send()

    for step in range(1, seq):
        for h in range(heads):
            grad_copy(h, lax.rem(s + step, seq), s).wait_send()
    for step in range(1, seq // 2):
        direct(step).wait_send()
    for step in range(seq // 2):
        forward(step).wait_send()


def backward(seq, dp, factor, packed, grad_y, w_rows):
    total = packed.shape[0]
    width, features = w_rows.shape
    heads = width // HEAD_DIM
    ratio = seq // dp
    piece = width // seq
    block_rows = 512
    while total % block_rows:
        block_rows //= 2
    dma = pltpu.SemaphoreType.DMA
    vmem = pl.BlockSpec(memory_space=pltpu.VMEM)
    hbm = pl.BlockSpec(memory_space=pl.ANY)
    low = pltpu.VMEM((heads, total, HEAD_DIM), jnp.bfloat16)
    wide = pltpu.VMEM((total, HEAD_DIM), jnp.float32)
    return pl.pallas_call(
        functools.partial(backward_kernel, seq, dp, heads, block_rows, factor),
        out_shape=(
            jax.ShapeDtypeStruct((heads, seq, total // seq, 3 * HEAD_DIM), jnp.bfloat16),
            jax.ShapeDtypeStruct((seq, ratio, piece, features), jnp.bfloat16),
        ),
        in_specs=[vmem] * 3,
        out_specs=(hbm, hbm),
        scratch_shapes=[
            low, low, low, low,
            pltpu.VMEM((heads, total // block_rows, 1, block_rows), jnp.float32),
            wide, wide,
            pltpu.VMEM((heads, total, 3 * HEAD_DIM), jnp.bfloat16),
            pltpu.VMEM((seq, piece, features), jnp.bfloat16),
            pltpu.VMEM((dp * ratio, piece, features), jnp.bfloat16),
            pltpu.VMEM((ratio, piece, features), jnp.bfloat16),
            dma((heads, seq)),
            dma((heads, seq)),
            dma((seq,)),
            dma((dp * ratio,)),
            dma((seq,)),
            dma((seq,)),
            dma((seq,)),
            dma((2 + heads,)),
        ],
        compiler_params=pltpu.CompilerParams(
            collective_id=1, has_side_effects=True, vmem_limit_bytes=VMEM_LIMIT
        ),
        name="attention_backward",
    )(packed, grad_y, w_rows)


def unpack_kernel(landed, spread, dq_ref, dk_ref, dv_ref, out_ref):
    heads, seq = landed.shape[:2]
    ratio, piece = spread.shape[1:3]
    width = heads * HEAD_DIM
    for source in range(seq):
        for h in range(heads):
            start = source * width + h * HEAD_DIM
            for index, ref in enumerate((dq_ref, dk_ref, dv_ref)):
                ref[:, start : start + HEAD_DIM] = landed[
                    h, source, :, index * HEAD_DIM : (index + 1) * HEAD_DIM
                ]
        for column in range(ratio):
            start = column * width + source * piece
            out_ref[start : start + piece, :] = spread[source, column].astype(jnp.float32)


def unpack(dp, landed, spread):
    rows = landed.shape[2]
    features = spread.shape[-1]
    vmem = pl.BlockSpec(memory_space=pltpu.VMEM)
    block = jax.ShapeDtypeStruct((rows, features), jnp.bfloat16)
    return pl.pallas_call(
        unpack_kernel,
        out_shape=(
            block, block, block,
            jax.ShapeDtypeStruct((features // dp, features), jnp.float32),
        ),
        in_specs=[vmem] * 2,
        out_specs=(vmem,) * 4,
        compiler_params=pltpu.CompilerParams(vmem_limit_bytes=VMEM_LIMIT),
        name="unpack",
    )(landed, spread)


def body(query, keys, values, attn, d_block, w_out):
    seq = lax.axis_size("seq")
    dp = lax.axis_size("dp")
    rows, features = query.shape[1:]
    width = features // seq
    flat = lambda array: array.reshape(rows, features)
    packed, grad_y, w_rows = gather(
        seq, dp, flat(query), flat(keys), flat(values), flat(attn), flat(d_block),
        w_out.reshape(seq // dp, width, features),
    )
    factor = 1.0 / float(dp * rows * seq) ** 0.5
    landed, spread = backward(
        seq, dp, factor,
        packed.reshape(seq * rows, 4 * width),
        grad_y.reshape(seq * rows, features),
        w_rows,
    )
    d_query, d_keys, d_values, d_weight = unpack(dp, landed, spread)
    whole = lambda array: array.reshape(1, rows, features)
    return whole(d_query), whole(d_keys), whole(d_values), d_weight


def solution(mesh):
    blocks = P("dp", "seq", None)
    return jax.shard_map(
        body,
        mesh=mesh,
        in_specs=(blocks,) * 5 + (P("dp", None),),
        out_specs=(blocks, blocks, blocks, P("dp", None)),
        check_vma=False,
    )
```

time: 139 us -> 118 us (0.85)
  Pallas kernels: 130 us -> 116 us
  local copies, waits for them, and re-layouts: 6.81 us -> 0 us
    pallas_call x2, Pallas kernels: 79.2 us -> 64.8 us  [the longest x1 60.4 us: backward(): pl.pallas_call(functools.partial(backward_kernel, seq, dp, heads, block_r...]
    unnamed x6 -> x0, local copies, waits for them, and re-layouts: 6.81 us -> none
where the time goes in v2:
time: 118 us; the launch traced here: 116 us
  Pallas kernels  116 us (98%)
    pallas_call x1, Pallas kernels, backward(): pl.pallas_call(functools.partial(backward_kernel, seq, dp, heads, block_r...  60.4 us
    pallas_call x1, Pallas kernels, gather(): pl.pallas_call(functools.partial(gather_kernel, seq, dp), out_shape=(jax....  51 us
    pallas_call x1, Pallas kernels, unpack(): pl.pallas_call(unpack_kernel, out_shape=(block, block, block, jax.ShapeDt...  4.41 us

profile of v2, /device:TPU:1, one launch (start us, length us, event | category | flops | bytes accessed | tf_op | source)
XLA Modules:
  0.0 116.5 jit_solution(313086070143838610)
XLA Ops:
  0.6 51.0 %gather_heads.1 = (bf16[8,192,640]{2,1,0:T(8,128)(2,1)}, bf16[8,192,1280]{2,1,0:T(8,128)(2,1)}, bf16[160,1280]{1,0:T(8,128)(2,1)}) custom-call(bf16[192,1280]{1,0:T(8,128)(2,1)} %bitcast.14, bf16[192,1280]{1,0:T(8,128)(2,1)} %bitcast.15, bf16[192,1280]{1,0:T(8,128)(2,1)} %bitcast.16, bf16[192,1280]{1,0:T(8,128)(2,1)} %bitcast.17, ...), custom_call_target="tpu_custom_call" | custom-call | tf_op jit(solution)/shard_map/gather_heads/pallas_call | solution.py:154
  51.6 60.4 %attention_backward.1 = (bf16[2,8,192,240]{3,2,1,0:T(8,128)(2,1)}, bf16[8,2,20,1280]{3,2,1,0:T(8,128)(2,1)}) custom-call(bf16[1536,640]{1,0:T(8,128)(2,1)} %bitcast.12, bf16[1536,1280]{1,0:T(8,128)(2,1)} %bitcast.11, bf16[160,1280]{1,0:T(8,128)(2,1)} %get-tuple-element.15.w_ref), custom_call_target="tpu_custom_call" | custom-call | tf_op jit(solution)/shard_map/attention_backward/pallas_call | solution.py:417
  112.1 4.4 %unpack.1 = (bf16[192,1280]{1,0:T(8,128)(2,1)}, bf16[192,1280]{1,0:T(8,128)(2,1)}, bf16[192,1280]{1,0:T(8,128)(2,1)}, f32[320,1280]{1,0:T(8,128)}) custom-call(bf16[2,8,192,240]{3,2,1,0:T(8,128)(2,1)} %get-tuple-element.16.landed, bf16[8,2,20,1280]{3,2,1,0:T(8,128)(2,1)} %get-tuple-element.17.spread), custom_call_target="tpu_custom_call" | custom-call | tf_op jit(solution)/shard_map/unpack/pallas_call | solution.py:470

commit v3 on v2

--- a/solution.py
+++ b/solution.py
@@ -9,6 +9,7 @@
 from jax.sharding import PartitionSpec as P
 
 HEAD_DIM = 80
+LANES = 128
 MESH = pl.DeviceIdType.MESH
 VMEM_LIMIT = 60 * 1024 * 1024
 LAST = (((1,), (1,)), ((), ()))
@@ -180,14 +181,12 @@
 
 def backward_kernel(
     seq, dp, heads, block_rows, factor, pack_ref, g_ref, w_ref, landed, spread,
-    q_s, k_s, v_s, do_s, delta_s, dk_s, dv_s, grad_s, dw_s, parts, total_s,
-    p_send, p_recv, w_send, w_recv, t_send, f_send, t_recv, local_sem,
+    q_s, k_s, v_s, do_s, delta_s, dk_s, dv_s, grad_s, dw_s, middle, parts, total_s,
+    p_send, p_recv, w_send, w_recv, z_send, z_recv, t_send, f_send, t_recv, local_sem,
 ):
     s = lax.axis_index("seq")
     d = lax.axis_index("dp")
     ratio = seq // dp
-    home = s // ratio
-    slot = d * ratio + s % ratio
     partner = s + 1 - 2 * (s % 2)
     patches = pack_ref.shape[0]
     rows_here = patches // seq
@@ -195,13 +194,23 @@
     scale = HEAD_DIM ** (-0.5)
     to_log2 = scale * math.log2(math.e)
 
-    def w_copy(peer):
+    def w_copy(peer, source):
         return pltpu.make_async_remote_copy(
             src_ref=dw_s.at[peer],
-            dst_ref=parts.at[slot],
+            dst_ref=middle.at[source],
             send_sem=w_send.at[peer],
-            recv_sem=w_recv.at[slot],
-            device_id=(peer, home),
+            recv_sem=w_recv.at[source],
+            device_id=(peer, d),
+            device_id_type=MESH,
+        )
+
+    def z_copy(plane, source):
+        return pltpu.make_async_remote_copy(
+            src_ref=middle.at[pl.ds(plane * ratio, ratio)],
+            dst_ref=parts.at[source],
+            send_sem=z_send.at[plane],
+            recv_sem=z_recv.at[source],
+            device_id=(s, plane),
             device_id_type=MESH,
         )
 
@@ -253,48 +262,59 @@
             device_id_type=MESH,
         ).wait_recv()
 
-    own_part = pltpu.make_async_copy(dw_s.at[s], parts.at[slot], local_sem.at[0])
+    own_middle = pltpu.make_async_copy(dw_s.at[s], middle.at[s], local_sem.at[0])
+    own_part = pltpu.make_async_copy(
+        middle.at[pl.ds(d * ratio, ratio)], parts.at[d], local_sem.at[2 + heads]
+    )
     own_total = pltpu.make_async_copy(total_s, spread.at[s], local_sem.at[1])
 
     barrier = pltpu.get_barrier_semaphore()
     for step in range(1, seq):
         pl.semaphore_signal(barrier, inc=1, device_id=(lax.rem(s + step, seq), d), device_id_type=MESH)
-    for row in range(dp):
-        for column in range(ratio):
-            @pl.when(jnp.logical_or(row != d, d * ratio + column != s))
-            def _():
-                pl.semaphore_signal(
-                    barrier, inc=1, device_id=(d * ratio + column, row), device_id_type=MESH
-                )
-
-    pieces = dw_s.shape[0]
-    piece = dw_s.shape[1]
+    for step in range(1, dp):
+        pl.semaphore_signal(barrier, inc=1, device_id=(s, lax.rem(d + step, dp)), device_id_type=MESH)
+
+    piece = width // seq
+    groups = g_ref.shape[1] // LANES
+    used = piece * groups
     d_weight = lax.dot_general(
         pack_ref[:, 3 * width : 4 * width], g_ref[...], FIRST, preferred_element_type=jnp.float32
     )
-    for index in range(pieces):
-        dw_s[index] = (d_weight[index * piece : (index + 1) * piece, :] * factor).astype(
-            jnp.bfloat16
-        )
-
-    @pl.when(home == d)
-    def _():
-        pl.semaphore_wait(barrier, 2 * seq - 2)
-
-    @pl.when(home != d)
-    def _():
-        pl.semaphore_wait(barrier, 2 * seq - 1)
-
-    for step in range(seq):
-        peer = lax.rem(s + step, seq)
-
-        @pl.when(jnp.logical_or(home != d, peer != s))
-        def _():
-            w_copy(peer).start()
-
-    @pl.when(home == d)
-    def _():
+    d_weight = d_weight * factor
+    for index in range(seq):
+        share = d_weight[index * piece : (index + 1) * piece, :]
+        tall = [share[:, group * LANES : (group + 1) * LANES] for group in range(groups)]
+        tall.append(jnp.zeros((dw_s.shape[1] - used, LANES), jnp.float32))
+        dw_s[index] = jnp.concatenate(tall, axis=0).astype(jnp.bfloat16)
+
+    pl.semaphore_wait(barrier, seq + dp - 2)
+    for step in range(1, seq):
+        w_copy(lax.rem(s + step, seq), s).start()
+    own_middle.start()
+
+    def relay():
+        own_middle.wait()
+        for step in range(1, seq):
+            source = lax.rem(s + seq - step, seq)
+            w_copy(source, source).wait_recv()
+        for step in range(1, dp):
+            z_copy(lax.rem(d + step, dp), d).start()
         own_part.start()
+
+    def combine():
+        own_part.wait()
+        for step in range(1, dp):
+            source = lax.rem(d + dp - step, dp)
+            z_copy(source, source).wait_recv()
+        for column in range(ratio):
+            value = parts[0, column].astype(jnp.float32)
+            for plane in range(1, dp):
+                value = value + parts[plane, column].astype(jnp.float32)
+            total_s[column] = value.astype(jnp.bfloat16)
+        for step in range(1, seq // 2):
+            direct(step).start()
+        forward(0).start()
+        own_total.start()
 
     @pl.loop(0, patches // block_rows)
     def _(block):
@@ -313,6 +333,7 @@
             product = do_h.astype(jnp.float32) * a_h.astype(jnp.float32)
             delta_s[h, block] = jnp.sum(product.T, axis=0, keepdims=True)
 
+    blocks = patches // block_rows
     for h in range(heads):
         dk_s[...] = jnp.zeros_like(dk_s)
         dv_s[...] = jnp.zeros_like(dv_s)
@@ -320,6 +341,10 @@
         @pl.loop(0, patches // block_rows)
         def _(block):
             rows = pl.ds(pl.multiple_of(block * block_rows, block_rows), block_rows)
+            if h == 0:
+                pl.when(block == min(1, blocks - 1))(relay)
+            if h == heads - 1:
+                pl.when(block == min(1 if heads > 1 else 2, blocks - 1))(combine)
             q_b = q_s[h, rows, :]
             do_b = do_s[h, rows, :]
             keys = k_s[h]
@@ -337,40 +362,9 @@
         grad_s[h, :, HEAD_DIM : 2 * HEAD_DIM] = dk_s[...].astype(jnp.bfloat16)
         grad_s[h, :, 2 * HEAD_DIM : 3 * HEAD_DIM] = dv_s[...].astype(jnp.bfloat16)
 
-        if h == 0:
-            for row in range(dp):
-                for column in range(ratio):
-                    source = row * ratio + column
-
-                    @pl.when(jnp.logical_or(row != d, d * ratio + column != s))
-                    def _():
-                        pltpu.make_async_remote_copy(
-                            src_ref=dw_s.at[0],
-                            dst_ref=parts.at[source],
-                            send_sem=w_send.at[0],
-                            recv_sem=w_recv.at[source],
-                            device_id=(d * ratio + column, row),
-                            device_id_type=MESH,
-                        ).wait_recv()
-
-            @pl.when(home == d)
-            def _():
-                own_part.wait()
-
-            for column in range(ratio):
-                value = parts[column].astype(jnp.float32)
-                for row in range(1, dp):
-                    value = value + parts[row * ratio + column].astype(jnp.float32)
-                total_s[column] = value.astype(jnp.bfloat16)
-
         for step in range(1, seq):
             grad_copy(h, lax.rem(s + step, seq), s).start()
         own_grad(h).start()
-        if h == 0:
-            for step in range(1, seq // 2):
-                direct(step).start()
-            forward(0).start()
-            own_total.start()
 
     for step in range(1, seq // 2):
         arrived(lax.rem(s + seq - 2 * step, seq))
@@ -384,12 +378,10 @@
         arrived(lax.rem(partner + seq - 2 * step, seq))
 
     own_total.wait()
-    for step in range(seq):
-        peer = lax.rem(s + step, seq)
-
-        @pl.when(jnp.logical_or(home != d, peer != s))
-        def _():
-            w_copy(peer).wait_send()
+    for step in range(1, seq):
+        w_copy(lax.rem(s + step, seq), s).wait_send()
+    for step in range(1, dp):
+        z_copy(lax.rem(d + step, dp), d).wait_send()
 
     for step in range(1, seq):
         for h in range(heads):
@@ -405,7 +397,7 @@
     width, features = w_rows.shape
     heads = width // HEAD_DIM
     ratio = seq // dp
-    piece = width // seq
+    tall = -(-(width // seq * features // LANES) // 16) * 16
     block_rows = 512
     while total % block_rows:
         block_rows //= 2
@@ -418,7 +410,7 @@
         functools.partial(backward_kernel, seq, dp, heads, block_rows, factor),
         out_shape=(
             jax.ShapeDtypeStruct((heads, seq, total // seq, 3 * HEAD_DIM), jnp.bfloat16),
-            jax.ShapeDtypeStruct((seq, ratio, piece, features), jnp.bfloat16),
+            jax.ShapeDtypeStruct((seq, ratio, tall, LANES), jnp.bfloat16),
         ),
         in_specs=[vmem] * 3,
         out_specs=(hbm, hbm),
@@ -427,17 +419,20 @@
             pltpu.VMEM((heads, total // block_rows, 1, block_rows), jnp.float32),
             wide, wide,
             pltpu.VMEM((heads, total, 3 * HEAD_DIM), jnp.bfloat16),
-            pltpu.VMEM((seq, piece, features), jnp.bfloat16),
-            pltpu.VMEM((dp * ratio, piece, features), jnp.bfloat16),
-            pltpu.VMEM((ratio, piece, features), jnp.bfloat16),
+            pltpu.VMEM((seq, tall, LANES), jnp.bfloat16),
+            pltpu.VMEM((seq, tall, LANES), jnp.bfloat16),
+            pltpu.VMEM((dp, ratio, tall, LANES), jnp.bfloat16),
+            pltpu.VMEM((ratio, tall, LANES), jnp.bfloat16),
             dma((heads, seq)),
             dma((heads, seq)),
             dma((seq,)),
-            dma((dp * ratio,)),
-            dma((seq,)),
-            dma((seq,)),
-            dma((seq,)),
-            dma((2 + heads,)),
+            dma((seq,)),
+            dma((dp,)),
+            dma((dp,)),
+            dma((seq,)),
+            dma((seq,)),
+            dma((seq,)),
+            dma((3 + heads,)),
         ],
         compiler_params=pltpu.CompilerParams(
             collective_id=1, has_side_effects=True, vmem_limit_bytes=VMEM_LIMIT
@@ -448,8 +443,10 @@
 
 def unpack_kernel(landed, spread, dq_ref, dk_ref, dv_ref, out_ref):
     heads, seq = landed.shape[:2]
-    ratio, piece = spread.shape[1:3]
+    ratio = spread.shape[1]
     width = heads * HEAD_DIM
+    piece = width // seq
+    groups = out_ref.shape[1] // LANES
     for source in range(seq):
         for h in range(heads):
             start = source * width + h * HEAD_DIM
@@ -459,12 +456,16 @@
                 ]
         for column in range(ratio):
             start = column * width + source * piece
-            out_ref[start : start + piece, :] = spread[source, column].astype(jnp.float32)
+            tall = spread[source, column].astype(jnp.float32)
+            for group in range(groups):
+                out_ref[start : start + piece, group * LANES : (group + 1) * LANES] = tall[
+                    group * piece : (group + 1) * piece
+                ]
 
 
 def unpack(dp, landed, spread):
     rows = landed.shape[2]
-    features = spread.shape[-1]
+    features = landed.shape[0] * landed.shape[1] * HEAD_DIM
     vmem = pl.BlockSpec(memory_space=pltpu.VMEM)
     block = jax.ShapeDtypeStruct((rows, features), jnp.bfloat16)
     return pl.pallas_call(

time: 118 us -> 98 us (0.83); the launches traced: 116 us -> 97.9 us
  Pallas kernels: 116 us -> 97.2 us
    pallas_call x1, Pallas kernels: 60.4 us -> 41.9 us  [backward(): pl.pallas_call(functools.partial(backward_kernel, seq, dp, heads, block_r...]
where the time goes in v3:
time: 98 us; the launch traced here: 97.9 us
  Pallas kernels  97.2 us (99%)
    pallas_call x1, Pallas kernels, gather(): pl.pallas_call(functools.partial(gather_kernel, seq, dp), out_shape=(jax....  51 us
    pallas_call x1, Pallas kernels, backward(): pl.pallas_call(functools.partial(backward_kernel, seq, dp, heads, block_r...  41.9 us
    pallas_call x1, Pallas kernels, unpack(): pl.pallas_call(unpack_kernel, out_shape=(block, block, block, jax.ShapeDt...  4.36 us

profile of v3, /device:TPU:1, one launch (start us, length us, event | category | flops | bytes accessed | tf_op | source)
XLA Modules:
  0.0 97.9 jit_solution(10055112232823098878)
XLA Ops:
  0.6 51.0 %gather_heads.1 = (bf16[8,192,640]{2,1,0:T(8,128)(2,1)}, bf16[8,192,1280]{2,1,0:T(8,128)(2,1)}, bf16[160,1280]{1,0:T(8,128)(2,1)}) custom-call(bf16[192,1280]{1,0:T(8,128)(2,1)} %bitcast.14, bf16[192,1280]{1,0:T(8,128)(2,1)} %bitcast.15, bf16[192,1280]{1,0:T(8,128)(2,1)} %bitcast.16, bf16[192,1280]{1,0:T(8,128)(2,1)} %bitcast.17, ...), custom_call_target="tpu_custom_call" | custom-call | tf_op jit(solution)/shard_map/gather_heads/pallas_call | solution.py:155
  51.6 41.9 %attention_backward.1 = (bf16[2,8,192,240]{3,2,1,0:T(8,128)(2,1)}, bf16[8,2,208,128]{3,2,1,0:T(8,128)(2,1)}) custom-call(bf16[1536,640]{1,0:T(8,128)(2,1)} %bitcast.12, bf16[1536,1280]{1,0:T(8,128)(2,1)} %bitcast.11, bf16[160,1280]{1,0:T(8,128)(2,1)} %get-tuple-element.15.w_ref), custom_call_target="tpu_custom_call" | custom-call | tf_op jit(solution)/shard_map/attention_backward/pallas_call | solution.py:409
  93.5 4.4 %unpack.1 = (bf16[192,1280]{1,0:T(8,128)(2,1)}, bf16[192,1280]{1,0:T(8,128)(2,1)}, bf16[192,1280]{1,0:T(8,128)(2,1)}, f32[320,1280]{1,0:T(8,128)}) custom-call(bf16[2,8,192,240]{3,2,1,0:T(8,128)(2,1)} %get-tuple-element.16.landed, bf16[8,2,208,128]{3,2,1,0:T(8,128)(2,1)} %get-tuple-element.17.spread), custom_call_target="tpu_custom_call" | custom-call | tf_op jit(solution)/shard_map/unpack/pallas_call | solution.py:471

commit v4 on v3

--- a/solution.py
+++ b/solution.py
@@ -398,7 +398,7 @@
     heads = width // HEAD_DIM
     ratio = seq // dp
     tall = -(-(width // seq * features // LANES) // 16) * 16
-    block_rows = 512
+    block_rows = 768
     while total % block_rows:
         block_rows //= 2
     dma = pltpu.SemaphoreType.DMA

time: 98 us -> 96.2 us (0.982)
  Pallas kernels: 97.2 us -> 95.4 us
    pallas_call x1, Pallas kernels: 41.9 us -> 40.1 us  [backward(): pl.pallas_call(functools.partial(backward_kernel, seq, dp, heads, block_r...]
where the time goes in v4:
time: 96.2 us; the launch traced here: 96.1 us
  Pallas kernels  95.4 us (99%)
    pallas_call x1, Pallas kernels, gather(): pl.pallas_call(functools.partial(gather_kernel, seq, dp), out_shape=(jax....  51 us
    pallas_call x1, Pallas kernels, backward(): pl.pallas_call(functools.partial(backward_kernel, seq, dp, heads, block_r...  40.1 us
    pallas_call x1, Pallas kernels, unpack(): pl.pallas_call(unpack_kernel, out_shape=(block, block, block, jax.ShapeDt...  4.36 us

profile of v4, /device:TPU:1, one launch (start us, length us, event | category | flops | bytes accessed | tf_op | source)
XLA Modules:
  0.0 96.1 jit_solution(16685886886405494058)
XLA Ops:
  0.6 51.0 %gather_heads.1 = (bf16[8,192,640]{2,1,0:T(8,128)(2,1)}, bf16[8,192,1280]{2,1,0:T(8,128)(2,1)}, bf16[160,1280]{1,0:T(8,128)(2,1)}) custom-call(bf16[192,1280]{1,0:T(8,128)(2,1)} %bitcast.14, bf16[192,1280]{1,0:T(8,128)(2,1)} %bitcast.15, bf16[192,1280]{1,0:T(8,128)(2,1)} %bitcast.16, bf16[192,1280]{1,0:T(8,128)(2,1)} %bitcast.17, ...), custom_call_target="tpu_custom_call" | custom-call | tf_op jit(solution)/shard_map/gather_heads/pallas_call | solution.py:155
  51.6 40.1 %attention_backward.1 = (bf16[2,8,192,240]{3,2,1,0:T(8,128)(2,1)}, bf16[8,2,208,128]{3,2,1,0:T(8,128)(2,1)}) custom-call(bf16[1536,640]{1,0:T(8,128)(2,1)} %bitcast.12, bf16[1536,1280]{1,0:T(8,128)(2,1)} %bitcast.11, bf16[160,1280]{1,0:T(8,128)(2,1)} %get-tuple-element.15.w_ref), custom_call_target="tpu_custom_call" | custom-call | tf_op jit(solution)/shard_map/attention_backward/pallas_call | solution.py:409
  91.7 4.4 %unpack.1 = (bf16[192,1280]{1,0:T(8,128)(2,1)}, bf16[192,1280]{1,0:T(8,128)(2,1)}, bf16[192,1280]{1,0:T(8,128)(2,1)}, f32[320,1280]{1,0:T(8,128)}) custom-call(bf16[2,8,192,240]{3,2,1,0:T(8,128)(2,1)} %get-tuple-element.16.landed, bf16[8,2,208,128]{3,2,1,0:T(8,128)(2,1)} %get-tuple-element.17.spread), custom_call_target="tpu_custom_call" | custom-call | tf_op jit(solution)/shard_map/unpack/pallas_call | solution.py:471
